TPU v7x, 32 devices: a whole 2x2x4 slice. The times are simulated.
32 devices in a mesh: seq: 16 (over z, x, core), pipe: 2 (over y).
Axes of the slice: x: 2, y: 2, z: 4, core: 2. Of those that a mesh axis runs over, the one named last changes fastest.
Arguments:
- queries: bfloat16 [2, 32, 2048, 128], P('pipe', None, 'seq'), may hold values from -160 to 160
- key_states: bfloat16 [2, 4, 2048, 128], P('pipe', None, 'seq'), may hold values from -5 to 5
- value_states: bfloat16 [2, 4, 2048, 128], P('pipe', None, 'seq'), may hold values from -6 to 6
- outputs: bfloat16 [2, 32, 2048, 128], P('pipe', None, 'seq'), may hold values from -6 to 6
- out_grads: bfloat16 [2, 32, 2048, 128], P('pipe', None, 'seq'), may hold values from -6 to 6
- selected: int32 [2, 4, 4, 2], P('pipe'), may hold values from 0 to 2, as said below
Outputs:
- grad_queries: bfloat16 [2, 32, 2048, 128], P('pipe', None, 'seq')
- grad_keys: bfloat16 [2, 4, 2048, 128], P('pipe', None, 'seq')
- grad_values: bfloat16 [2, 4, 2048, 128], P('pipe', None, 'seq')
Inputs may be any that keep to these rules, and one draw needn't show every extreme that they name: `selected`: for every block b of 2 or more and every key head the two entries are different blocks below b. For block 1 the entries are 0 and 1, for block 0 both are 0. An entry that is not below its block's index stands for no block.
All inputs are finite; a program needn't handle non-finite values.
Results may differ from a plain program's by a relative error of at most 0.009.
Values may be sent and summed in bfloat16 or wider, within the bound.
No kernel may reach another device: no remote copies, remote signals or barrier semaphores. Data moves between devices by JAX's collectives and lax.ppermute only.
A program may use at most 64 MiB of HBM per device.

v0:
```python
import functools
import math

import jax
import jax.numpy as jnp
from jax import lax
from jax.experimental import pallas as pl
from jax.experimental.pallas import tpu as pltpu
from jax.sharding import PartitionSpec as P

BLK = 512
TILE_HEADS = 4
FAR = 1e30


def nt(a, b):
    return lax.dot_general(a, b, (((1,), (1,)), ((), ())), preferred_element_type=jnp.float32)


def nn(a, b):
    return lax.dot_general(a, b, (((1,), (0,)), ((), ())), preferred_element_type=jnp.float32)


def tn(a, b):
    return lax.dot_general(a, b, (((0,), (0,)), ((), ())), preferred_element_type=jnp.float32)


def attend_kernel(sizes, first, meta, *refs):
    members, reach, heads, rows, feature = sizes
    take = list(refs)
    if first:
        queries, grads, deltas, pack = take[:4]
        near, far, take = take[4], take[5 : 5 + reach], take[5 + reach :]
        query_outs, acc_outs, take = take[:2], take[2:4], take[4:]
    else:
        packs, acc_ins = take[:2], take[2:4]
        near, far, take = take[4], take[5 : 5 + reach], take[5 + reach :]
        query_outs, take = take[:2], take[2:]
        far_outs, own_out, take = take[:reach], take[reach], take[reach + 1 :]
    query_buf, grad_buf, low_buf, delta_buf, pair_buf, key_acc, value_acc, query_done = take[:8]
    in_sem, pair_sem, out_sem = take[8:11]
    mine = meta[0]
    offsets = (meta[1], meta[2])
    lanes = TILE_HEADS * rows
    factor = feature ** (-0.5)
    sharp = factor * math.log2(math.e)
    group = mine // 2 if first else 1 - mine // 2
    places = [mine % 2, 1 - mine % 2]

    def run(pairs, sems):
        copies = [
            pltpu.make_async_copy(source, target, sems.at[i])
            for i, (source, target) in enumerate(pairs)
        ]
        for copy in copies:
            copy.start()
        return copies

    def of_pack(pack, place):
        return [
            (pack.at[pl.ds(0, heads)], query_buf.at[place]),
            (pack.at[pl.ds(heads, heads)], grad_buf.at[place]),
            (pack.at[2 * heads, pl.ds(0, 16)], low_buf.at[place]),
        ]

    loads = [(near.at[:, hop], pair_buf.at[2, :, mine ^ hop]) for hop in range(members)]
    if first:
        span = pl.ds(mine * heads, heads)
        loads += [
            (queries.at[0, span], query_buf.at[places[0]]),
            (grads.at[0, span], grad_buf.at[places[0]]),
            (deltas.at[mine], low_buf.at[places[0]]),
        ]
        loads += of_pack(pack, places[1])
        key_acc[...] = jnp.zeros_like(key_acc)
        value_acc[...] = jnp.zeros_like(value_acc)
    else:
        loads += of_pack(packs[0], places[0]) + of_pack(packs[1], places[1])
        loads += [(acc_ins[0], key_acc), (acc_ins[1], value_acc)]
    copies = run(loads, in_sem)
    for slot in range(2):
        for hop in range(reach + 1):
            source = near if hop == 0 else far[hop - 1]

            @pl.when(offsets[slot] == hop)
            def _(source=source, slot=slot):
                pltpu.make_async_copy(source, pair_buf.at[slot], pair_sem.at[slot]).start()

    for copy in copies:
        copy.wait()
    for slot in range(2):
        pltpu.make_async_copy(near, pair_buf.at[slot], pair_sem.at[slot]).wait()
    delta_buf[...] = low_buf[...].astype(jnp.float32)

    biases = [jnp.where(offset > 0, 0.0, FAR) for offset in offsets]

    steps = heads // TILE_HEADS
    edge_rows = 2 * rows

    def spans_of(half):
        return ((0, BLK), (1, BLK), (2, (half + 1) * edge_rows))

    def fetch(part, slot, length):
        return pair_buf[slot, part].reshape(members * rows, feature)[:length]

    def rows_of(buffer, place, step):
        return buffer[place, pl.ds(step * TILE_HEADS, TILE_HEADS)].reshape(lanes, feature)

    def score(half, place, step):
        query = rows_of(query_buf, place, step)
        return [nt(fetch(0, slot, length), query) for slot, length in spans_of(half)]

    def soften(half, place, scores):
        key_ids = lax.broadcasted_iota(jnp.int32, (edge_rows, lanes), 0)
        row_ids = lax.broadcasted_iota(jnp.int32, (edge_rows, lanes), 1) % rows
        fixed = half * edge_rows
        edge = jnp.where(key_ids <= row_ids + place * rows, scores[2][fixed:], -FAR)
        scores[2] = jnp.concatenate([scores[2][:fixed], edge], axis=0) if half else edge
        tops = [jnp.max(part, axis=0, keepdims=True) for part in scores]
        top = jnp.maximum(jnp.maximum(tops[0] - biases[0], tops[1] - biases[1]), tops[2])
        shifts = [top + biases[0], top + biases[1], top]
        raws = [jnp.exp2((part - shift) * sharp) for part, shift in zip(scores, shifts)]
        total = sum(jnp.sum(raw, axis=0, keepdims=True) for raw in raws)
        return raws, 1.0 / total

    def spread(half, place, step, raws, inverse):
        query = rows_of(query_buf, place, step)
        grad = rows_of(grad_buf, place, step)
        delta = jnp.concatenate(
            [
                delta_buf[place, pl.ds(step * TILE_HEADS + i, 1), :]
                for i in range(TILE_HEADS)
            ],
            axis=1,
        )
        query_sum = jnp.zeros((lanes, feature), jnp.float32)
        for (slot, length), raw in zip(spans_of(half), raws):
            dprobs = nt(fetch(1, slot, length), grad)
            probs = raw * inverse
            dscores = (probs * (dprobs - delta)).astype(jnp.bfloat16)
            base = slot * BLK
            value_acc[base : base + length] += nn(probs.astype(jnp.bfloat16), grad)
            key_acc[base : base + length] += nn(dscores, query)
            query_sum += tn(dscores, fetch(0, slot, length))
        query_done[place, pl.ds(step * TILE_HEADS, TILE_HEADS)] = (
            (query_sum * factor).astype(jnp.bfloat16).reshape(TILE_HEADS, rows, feature)
        )

    for half in range(members // 2):

        @pl.when(group == half)
        def _(half=half):
            def tile(index, carry, half=half):
                place, step = index // steps, index % steps
                raws, inverse = soften(half, place, score(half, place, step))
                spread(half, place, step, raws, inverse)
                return carry

            lax.fori_loop(0, 2 * steps, tile, 0)

    stores = [(query_done.at[place], out) for place, out in zip(places, query_outs)]
    if first:
        copies = run(stores + [(key_acc, acc_outs[0]), (value_acc, acc_outs[1])], out_sem)
        for copy in copies:
            copy.wait()
        return
    far_done, own_done, blank, far_sem = take[11:]
    copies = run(stores, out_sem)
    blank[...] = jnp.zeros_like(blank)
    shape = (members, rows, feature)
    for slot in range(2):
        span = slice(slot * BLK, (slot + 1) * BLK)
        far_done[slot, 0] = (key_acc[span] * factor).astype(jnp.bfloat16).reshape(shape)
        far_done[slot, 1] = value_acc[span].astype(jnp.bfloat16).reshape(shape)
    for hop in range(1, reach + 1):
        target = far_outs[hop - 1]
        for slot in range(2):

            @pl.when(offsets[slot] == hop)
            def _(target=target, slot=slot, hop=hop):
                pltpu.make_async_copy(far_done.at[slot], target, far_sem.at[hop]).start()

        @pl.when((offsets[0] != hop) & (offsets[1] != hop))
        def _(target=target, hop=hop):
            pltpu.make_async_copy(blank, target, far_sem.at[hop]).start()

    own_done[0] = (key_acc[2 * BLK :] * factor).reshape(shape)
    own_done[1] = value_acc[2 * BLK :].reshape(shape)
    for hop in range(members):
        copy = pltpu.make_async_copy(
            own_done.at[:, mine ^ hop], own_out.at[:, hop], out_sem.at[2 + hop]
        )
        copy.start()
        copies.append(copy)
    for copy in copies:
        copy.wait()
    for hop in range(1, reach + 1):
        pltpu.make_async_copy(blank, far_outs[hop - 1], far_sem.at[hop]).wait()


def attend(meta, inputs, near, far, sizes, first):
    members, reach, heads, rows, feature = sizes
    low, wide = jnp.bfloat16, jnp.float32
    pair = (2, members, rows, feature)
    acc = (3 * BLK, feature)
    anywhere = pl.BlockSpec(memory_space=pl.ANY)
    outs = [jax.ShapeDtypeStruct((heads, rows, feature), low)] * 2
    scratch = [
        pltpu.VMEM((2, heads, rows, feature), low),
        pltpu.VMEM((2, heads, rows, feature), low),
        pltpu.VMEM((2, 16, rows), low),
        pltpu.VMEM((2, 16, rows), wide),
        pltpu.VMEM((3,) + pair, low),
        pltpu.VMEM(acc, wide),
        pltpu.VMEM(acc, wide),
        pltpu.VMEM((2, heads, rows, feature), low),
        pltpu.SemaphoreType.DMA((members + 8,)),
        pltpu.SemaphoreType.DMA((2,)),
        pltpu.SemaphoreType.DMA((members + 2,)),
    ]
    if first:
        outs += [jax.ShapeDtypeStruct(acc, wide)] * 2
    else:
        outs += [jax.ShapeDtypeStruct(pair, low)] * reach + [jax.ShapeDtypeStruct(pair, wide)]
        scratch += [
            pltpu.VMEM((2,) + pair, low),
            pltpu.VMEM(pair, wide),
            pltpu.VMEM(pair, low),
            pltpu.SemaphoreType.DMA((reach + 1,)),
        ]
    work = heads * 2 * rows * (2 * BLK + 3 * rows)
    return pl.pallas_call(
        functools.partial(attend_kernel, sizes, first),
        out_shape=outs,
        in_specs=[pl.BlockSpec(memory_space=pltpu.SMEM)]
        + [anywhere] * (len(inputs) + 1 + reach),
        out_specs=[anywhere] * len(outs),
        scratch_shapes=scratch,
        cost_estimate=pl.CostEstimate(
            flops=10 * work * feature, transcendentals=work, bytes_accessed=6 * 1024 * 1024
        ),
        compiler_params=pltpu.CompilerParams(vmem_limit_bytes=48 * 1024 * 1024),
    )(meta, *inputs, near, *far)


def settle_kernel(members, heads, meta, *refs):
    query_parts, pair_parts = refs[:members], refs[members : 2 * members]
    query_out, key_out, value_out, sem = refs[2 * members :]
    mine = meta[0]
    copies = []
    for hop in range(members):
        owner = mine ^ hop
        for source, target in (
            (query_parts[hop], query_out.at[0, pl.ds(owner * heads, heads)]),
            (pair_parts[hop].at[0], key_out.at[0, owner]),
            (pair_parts[hop].at[1], value_out.at[0, owner]),
        ):
            copy = pltpu.make_async_copy(source, target, sem)
            copy.start()
            copies.append(copy)
    for copy in copies:
        copy.wait()


def settle(meta, query_parts, pair_parts, shapes):
    members = len(query_parts)
    heads = query_parts[0].shape[0]
    anywhere = pl.BlockSpec(memory_space=pl.ANY)
    return pl.pallas_call(
        functools.partial(settle_kernel, members, heads),
        out_shape=[jax.ShapeDtypeStruct(shape, jnp.bfloat16) for shape in shapes],
        in_specs=[pl.BlockSpec(memory_space=pltpu.SMEM)]
        + [pl.BlockSpec(memory_space=pltpu.VMEM)] * (2 * members),
        out_specs=[anywhere] * 3,
        scratch_shapes=[pltpu.SemaphoreType.DMA],
    )(meta, *query_parts, *pair_parts)


def on_device(queries, key_states, value_states, outputs, out_grads, selected):
    devices = lax.axis_size("seq")
    sections = lax.axis_size("pipe")
    head_count, rows, feature = queries.shape[1:]
    key_heads = key_states.shape[1]
    members = BLK // rows
    heads = head_count // key_heads
    reach = devices // members - 1
    assert members == 4 and key_heads == 4 and heads <= 16
    rank = lax.axis_index("seq")
    mine = rank % members
    block = rank // members

    def around(tensor, hop):
        return lax.ppermute(tensor, "seq", [(i, i ^ hop) for i in range(devices)])

    def along(tensor, hop):
        step = members * hop
        route = [(i, i + step) for i in range(devices) if 0 <= i + step < devices]
        return lax.ppermute(tensor, "seq", route)

    def previous(tensor, hop):
        route = [
            (i * sections + s, (i ^ hop) * sections + s - 1)
            for i in range(devices)
            for s in range(1, sections)
        ]
        return lax.ppermute(tensor, ("seq", "pipe"), route)

    chosen = lax.dynamic_slice(selected, (0, block, mine, 0), (1, 1, 1, 2)).reshape(2)
    usable = chosen < block
    offsets = jnp.where(usable, block - chosen, 0)
    meta = jnp.concatenate([mine[None], offsets]).astype(jnp.int32)

    def pair_of(hop):
        return jnp.concatenate(
            [
                lax.dynamic_slice_in_dim(states[0], mine ^ hop, 1, 0)
                for states in (key_states, value_states)
            ],
            axis=0,
        )

    deltas = jnp.sum(
        out_grads[0].astype(jnp.float32) * outputs[0].astype(jnp.float32), axis=-1
    ).astype(jnp.bfloat16)
    deltas = deltas.reshape(key_heads, heads, rows)
    deltas = jnp.pad(deltas, ((0, 0), (0, 16 - heads), (0, 0)))

    def pack_of(hop):
        other = mine ^ hop
        query_part = lax.dynamic_slice_in_dim(queries[0], other * heads, heads, 0)
        grad_part = lax.dynamic_slice_in_dim(out_grads[0], other * heads, heads, 0)
        extra = lax.dynamic_index_in_dim(deltas, other, axis=0, keepdims=True)
        extra = jnp.pad(extra, ((0, 0), (0, rows - 16), (0, 0)))
        if hop == 1:
            extra = lax.optimization_barrier(jnp.concatenate([extra, pair_of(hop)], axis=0))
        return jnp.concatenate([query_part, grad_part, extra], axis=0)

    sides = [around(pair_of(hop), hop) for hop in range(2, members)]
    packs = [around(pack_of(hop), hop) for hop in range(1, members)]
    pieces = [pair_of(0), packs[0][2 * heads + 1 :]] + sides
    near = jnp.stack(pieces, axis=1)
    far = [along(near, hop) for hop in range(1, reach + 1)]

    sizes = (members, reach, heads, rows, feature)
    inputs = [queries, out_grads, deltas, packs[0]]
    *early_parts, key_acc, value_acc = attend(meta, inputs, near, far, sizes, True)
    early = [previous(part, hop) for hop, part in enumerate(early_parts)]
    inputs = [packs[1], packs[2], key_acc, value_acc]
    results = attend(meta, inputs, near, far, sizes, False)
    late_parts, far_parts, own_part = results[:2], results[2:-1], results[-1]
    early, late_parts, far_parts = lax.optimization_barrier((early, late_parts, far_parts))
    far_back = [along(part, -hop - 1) for hop, part in enumerate(far_parts)]
    late = [previous(part, hop + 2) for hop, part in enumerate(late_parts)]
    summed = own_part
    for part in far_back:
        summed = summed + part.astype(jnp.float32)
    summed = summed.astype(jnp.bfloat16)
    pair_back = [previous(summed[:, hop], hop) for hop in range(members)]
    shapes = (queries.shape, key_states.shape, value_states.shape)
    return tuple(settle(meta, early + late, pair_back, shapes))


def solution(mesh):
    return jax.shard_map(
        on_device,
        mesh=mesh,
        in_specs=(
            P("pipe", None, "seq", None),
            P("pipe", None, "seq", None),
            P("pipe", None, "seq", None),
            P("pipe", None, "seq", None),
            P("pipe", None, "seq", None),
            P("pipe", None, None, None),
        ),
        out_specs=(
            P("pipe", None, "seq", None),
            P("pipe", None, "seq", None),
            P("pipe", None, "seq", None),
        ),
        check_vma=False,
    )
```

profile of v0, /device:TPU:8, one launch (start us, length us, event | category | flops | bytes accessed | tf_op | source)
XLA Modules:
  0.0 101.1 jit_solution(8391914671885475944)
XLA Ops:
  0.7 0.0 copy-start.7
  0.7 0.0 copy-start.8
  0.7 0.0 copy-start
  0.7 0.0 copy-start.1
  0.7 2.3 %multiply_reduce_fusion = bf16[32,128]{1,0:T(8,128)(2,1)S(1)} fusion(bf16[1,32,128,128]{3,2,1,0:T(8,128)(2,1)} %param.9, bf16[1,32,128,128]{3,2,1,0:T(8,128)(2,1)} %refs_1_.1), kind=kLoop, calls=%fused_computation | loop fusion | flops 2093056 | bytes 2105344 | tf_op jit(solution)/shard_map/reduce_sum | solution.py:322
  3.1 0.0 copy-done.7
  3.1 0.0 copy-done.8
  3.2 0.0 copy-done
  3.2 0.0 copy-done.1
  3.2 0.1 dynamic-slice_bitcast_fusion
  3.3 0.1 pad_maximum_fusion
  3.4 0.1 collective-permute-start
  3.5 1.6 %collective-permute-start.2 = (bf16[2,128,128]{2,1,0:T(8,128)(2,1)S(1)}, bf16[2,128,128]{2,1,0:T(8,128)(2,1)S(1)}, u32[]{:S(2)}, u32[]{:S(2)}) collective-permute-start(bf16[2,128,128]{2,1,0:T(8,128)(2,1)S(1)} %pad_maximum_fusion.3), channel_id=1, source_target_pairs={{0,6},{2,4},{4,2},{6,0},{8,14},{10,12},{12,10},{14,8},{16,22},{18,... | collective-permute-start | bytes 196616 | tf_op jit(solution)/shard_map/ppermute | solution.py:293
  5.2 0.6 collective-permute-start.1
  5.7 0.9 fusion.2
  6.6 1.5 %collective-permute-start.8 = (bf16[17,128,128]{2,1,0:T(8,128)(2,1)}, bf16[17,128,128]{2,1,0:T(8,128)(2,1)}, u32[]{:S(2)}, u32[]{:S(2)}) collective-permute-start(bf16[17,128,128]{2,1,0:T(8,128)(2,1)} %fusion.2), channel_id=1, source_target_pairs={{0,4},{2,6},{4,0},{6,2},{8,12},{10,14},{12,8},{14,10},{16,20},{18,... | collective-permute-start | bytes 1671176 | tf_op jit(solution)/shard_map/ppermute | solution.py:293
  8.1 0.0 collective-permute-done.refs_3_
  8.1 0.0 collective-permute-done.2
  8.1 1.7 %collective-permute-done.1 = bf16[2,128,128]{2,1,0:T(8,128)(2,1)S(1)} collective-permute-done((bf16[2,128,128]{2,1,0:T(8,128)(2,1)S(1)}, bf16[2,128,128]{2,1,0:T(8,128)(2,1)S(1)}, u32[]{:S(2)}, u32[]{:S(2)}) %collective-permute-start.1) | collective-permute-done | bytes 65568 | tf_op jit(solution)/shard_map/ppermute | solution.py:293
  9.9 3.5 %collective-permute-start.3 = (bf16[2,4,128,128]{3,2,1,0:T(8,128)(2,1)S(1)}, bf16[2,4,128,128]{3,2,1,0:T(8,128)(2,1)S(1)}, u32[]{:S(2)}, u32[]{:S(2)}) collective-permute-start(bf16[2,4,128,128]{3,2,1,0:T(8,128)(2,1)S(1)} %pad_maximum_fusion.1.refs_4_), channel_id=1, source_target_pairs={{0,8},{2,10},{4,12},{6,14},{8,16},{10,18},{12,20},{14,22},{16,24},... | collective-permute-start | bytes 786440 | tf_op jit(solution)/shard_map/ppermute | solution.py:298
  13.4 2.3 %collective-permute-start.4 = (bf16[2,4,128,128]{3,2,1,0:T(8,128)(2,1)S(1)}, bf16[2,4,128,128]{3,2,1,0:T(8,128)(2,1)S(1)}, u32[]{:S(2)}, u32[]{:S(2)}) collective-permute-start(bf16[2,4,128,128]{3,2,1,0:T(8,128)(2,1)S(1)} %pad_maximum_fusion.1.refs_4_), channel_id=1, source_target_pairs={{0,16},{2,18},{4,20},{6,22},{8,24},{10,26},{12,28},{14,30},{1,17},... | collective-permute-start | bytes 786440 | tf_op jit(solution)/shard_map/ppermute | solution.py:298
  15.7 1.4 %collective-permute-start.5 = (bf16[2,4,128,128]{3,2,1,0:T(8,128)(2,1)S(1)}, bf16[2,4,128,128]{3,2,1,0:T(8,128)(2,1)}, u32[]{:S(2)}, u32[]{:S(2)}) collective-permute-start(bf16[2,4,128,128]{3,2,1,0:T(8,128)(2,1)S(1)} %pad_maximum_fusion.1.refs_4_), channel_id=1, source_target_pairs={{0,24},{2,26},{4,28},{6,30},{1,25},{3,27},{5,29},{7,31}} | collective-permute-start | bytes 786440 | tf_op jit(solution)/shard_map/ppermute | solution.py:298
  17.1 0.9 fusion.3
  18.0 0.0 collective-permute-start.9
  18.0 0.9 fusion.10
  18.8 0.1 pad_add_fusion.meta
  18.9 12.5 %collective-permute-done.3.refs_5_ = bf16[2,4,128,128]{3,2,1,0:T(8,128)(2,1)S(1)} collective-permute-done((bf16[2,4,128,128]{3,2,1,0:T(8,128)(2,1)S(1)}, bf16[2,4,128,128]{3,2,1,0:T(8,128)(2,1)S(1)}, u32[]{:S(2)}, u32[]{:S(2)}) %collective-permute-start.3) | collective-permute-done | bytes 262176 | tf_op jit(solution)/shard_map/ppermute | solution.py:298
  31.4 3.2 %collective-permute-done.4.refs_6_ = bf16[2,4,128,128]{3,2,1,0:T(8,128)(2,1)S(1)} collective-permute-done((bf16[2,4,128,128]{3,2,1,0:T(8,128)(2,1)S(1)}, bf16[2,4,128,128]{3,2,1,0:T(8,128)(2,1)S(1)}, u32[]{:S(2)}, u32[]{:S(2)}) %collective-permute-start.4) | collective-permute-done | bytes 262176 | tf_op jit(solution)/shard_map/ppermute | solution.py:298
  34.6 0.0 collective-permute-done.5.refs_7_
  34.6 10.9 %shard_map.85 = (bf16[8,128,128]{2,1,0:T(8,128)(2,1)S(1)}, bf16[8,128,128]{2,1,0:T(8,128)(2,1)S(1)}, f32[1536,128]{1,0:T(8,128)S(1)}, f32[1536,128]{1,0:T(8,128)S(1)}) custom-call(s32[3]{0:T(128)S(1)} %pad_add_fusion.meta, bf16[1,32,128,128]{3,2,1,0:T(8,128)(2,1)S(1)} %copy-done.1, bf16[1,32,128,128]{3,2,1,0:T(8,128)(2,1)S(1)} %copy-done, ...), custom_call_target="tpu_custom_call" | custom-call | flops 3690987520 | bytes 6291456 | tf_op jit(solution)/shard_map/pallas_call | solution.py:232
  45.5 1.3 %collective-permute-start.6 = (bf16[8,128,128]{2,1,0:T(8,128)(2,1)S(1)}, bf16[8,128,128]{2,1,0:T(8,128)(2,1)S(1)}, u32[]{:S(2)}, u32[]{:S(2)}) collective-permute-start(bf16[8,128,128]{2,1,0:T(8,128)(2,1)S(1)} %get-tuple-element.20), channel_id=1, source_target_pairs={{1,0},{3,2},{5,4},{7,6},{9,8},{11,10},{13,12},{15,14},{17,16},{19,... | collective-permute-start | bytes 786440 | tf_op jit(solution)/shard_map/ppermute | solution.py:306
  46.8 1.3 %collective-permute-start.7 = (bf16[8,128,128]{2,1,0:T(8,128)(2,1)S(1)}, bf16[8,128,128]{2,1,0:T(8,128)(2,1)S(1)}, u32[]{:S(2)}, u32[]{:S(2)}) collective-permute-start(bf16[8,128,128]{2,1,0:T(8,128)(2,1)S(1)} %get-tuple-element.21), channel_id=1, source_target_pairs={{1,2},{3,0},{5,6},{7,4},{9,10},{11,8},{13,14},{15,12},{17,18},{19,... | collective-permute-start | bytes 786440 | tf_op jit(solution)/shard_map/ppermute | solution.py:306
  48.1 0.0 collective-permute-done.8.refs_0_
  48.1 0.0 collective-permute-done.9.refs_1_
  48.1 0.0 copy-done.2
  48.2 14.3 %shard_map.86 = (bf16[8,128,128]{2,1,0:T(8,128)(2,1)S(1)}, bf16[8,128,128]{2,1,0:T(8,128)(2,1)S(1)}, bf16[2,4,128,128]{3,2,1,0:T(8,128)(2,1)S(1)}, bf16[2,4,128,...) custom-call(s32[3]{0:T(128)S(1)} %pad_add_fusion.meta, ...), custom_call_target="tpu_custom_call" | custom-call | flops 3690987520 | bytes 6291456 | tf_op jit(solution)/shard_map/pallas_call | solution.py:232
  62.5 0.0 collective-permute-done.6.refs_0_
  62.5 0.0 copy-start.3
  62.5 0.0 collective-permute-done.7.refs_1_
  62.5 0.0 copy-start.4
  62.5 0.7 collective-permute-start.14
  63.3 1.3 %collective-permute-start.13 = (bf16[2,4,128,128]{3,2,0,1:T(8,128)(2,1)S(1)}, bf16[2,4,128,128]{3,2,0,1:T(8,128)(2,1)S(1)}, u32[]{:S(2)}, u32[]{:S(2)}) collective-permute-start(bf16[2,4,128,128]{3,2,0,1:T(8,128)(2,1)S(1)} %copy.11), channel_id=1, source_target_pairs={{16,0},{18,2},{20,4},{22,6},{24,8},{26,10},{28,12},{30,14},{17,1},... | collective-permute-start | bytes 786440 | tf_op jit(solution)/shard_map/ppermute | solution.py:298
  64.6 1.9 %collective-permute-start.12 = (bf16[2,4,128,128]{3,2,0,1:T(8,128)(2,1)S(1)}, bf16[2,4,128,128]{3,2,0,1:T(8,128)(2,1)S(1)}, u32[]{:S(2)}, u32[]{:S(2)}) collective-permute-start(bf16[2,4,128,128]{3,2,0,1:T(8,128)(2,1)S(1)} %copy.9), channel_id=1, source_target_pairs={{8,0},{10,2},{12,4},{14,6},{16,8},{18,10},{20,12},{22,14},{24,16},... | collective-permute-start | bytes 786440 | tf_op jit(solution)/shard_map/ppermute | solution.py:298
  66.5 1.3 %collective-permute-start.10 = (bf16[8,128,128]{2,1,0:T(8,128)(2,1)S(1)}, bf16[8,128,128]{2,1,0:T(8,128)(2,1)S(1)}, u32[]{:S(2)}, u32[]{:S(2)}) collective-permute-start(bf16[8,128,128]{2,1,0:T(8,128)(2,1)S(1)} %get-tuple-element.31), channel_id=1, source_target_pairs={{1,4},{3,6},{5,0},{7,2},{9,12},{11,14},{13,8},{15,10},{17,20},{19,... | collective-permute-start | bytes 786440 | tf_op jit(solution)/shard_map/ppermute | solution.py:306
  67.8 1.3 %collective-permute-start.11 = (bf16[8,128,128]{2,1,0:T(8,128)(2,1)S(1)}, bf16[8,128,128]{2,1,0:T(8,128)(2,1)S(1)}, u32[]{:S(2)}, u32[]{:S(2)}) collective-permute-start(bf16[8,128,128]{2,1,0:T(8,128)(2,1)S(1)} %get-tuple-element.32), channel_id=1, source_target_pairs={{1,6},{3,4},{5,2},{7,0},{9,14},{11,12},{13,10},{15,8},{17,22},{19,... | collective-permute-start | bytes 786440 | tf_op jit(solution)/shard_map/ppermute | solution.py:306
  69.1 0.0 collective-permute-done.14
  69.1 10.7 %collective-permute-done.13 = bf16[2,4,128,128]{3,2,0,1:T(8,128)(2,1)S(1)} collective-permute-done((bf16[2,4,128,128]{3,2,0,1:T(8,128)(2,1)S(1)}, bf16[2,4,128,128]{3,2,0,1:T(8,128)(2,1)S(1)}, u32[]{:S(2)}, u32[]{:S(2)}) %collective-permute-start.13) | collective-permute-done | bytes 262176 | tf_op jit(solution)/shard_map/ppermute | solution.py:298
  79.9 5.2 %collective-permute-done.12 = bf16[2,4,128,128]{3,2,0,1:T(8,128)(2,1)S(1)} collective-permute-done((bf16[2,4,128,128]{3,2,0,1:T(8,128)(2,1)S(1)}, bf16[2,4,128,128]{3,2,0,1:T(8,128)(2,1)S(1)}, u32[]{:S(2)}, u32[]{:S(2)}) %collective-permute-start.12) | collective-permute-done | bytes 262176 | tf_op jit(solution)/shard_map/ppermute | solution.py:298
  85.1 0.1 fusion.6
  85.2 0.0 copy-done.3
  85.3 1.3 %collective-permute-start.15 = (bf16[2,128,128]{2,1,0:T(8,128)(2,1)S(1)}, bf16[2,128,128]{2,1,0:T(8,128)(2,1)S(1)}, u32[]{:S(2)}, u32[]{:S(2)}) collective-permute-start(bf16[2,128,128]{2,1,0:T(8,128)(2,1)S(1)} %get-tuple-element.46), channel_id=1, source_target_pairs={{1,0},{3,2},{5,4},{7,6},{9,8},{11,10},{13,12},{15,14},{17,16},{19,... | collective-permute-start | bytes 196616 | tf_op jit(solution)/shard_map/ppermute | solution.py:306
  86.6 1.3 %collective-permute-start.16 = (bf16[2,128,128]{2,1,0:T(8,128)(2,1)S(1)}, bf16[2,128,128]{2,1,0:T(8,128)(2,1)S(1)}, u32[]{:S(2)}, u32[]{:S(2)}) collective-permute-start(bf16[2,128,128]{2,1,0:T(8,128)(2,1)S(1)} %get-tuple-element.45), channel_id=1, source_target_pairs={{1,2},{3,0},{5,6},{7,4},{9,10},{11,8},{13,14},{15,12},{17,18},{19,... | collective-permute-start | bytes 196616 | tf_op jit(solution)/shard_map/ppermute | solution.py:306
  87.9 1.3 %collective-permute-start.17 = (bf16[2,128,128]{2,1,0:T(8,128)(2,1)S(1)}, bf16[2,128,128]{2,1,0:T(8,128)(2,1)S(1)}, u32[]{:S(2)}, u32[]{:S(2)}) collective-permute-start(bf16[2,128,128]{2,1,0:T(8,128)(2,1)S(1)} %get-tuple-element.44), channel_id=1, source_target_pairs={{1,4},{3,6},{5,0},{7,2},{9,12},{11,14},{13,8},{15,10},{17,20},{19,... | collective-permute-start | bytes 196616 | tf_op jit(solution)/shard_map/ppermute | solution.py:306
  89.2 0.0 collective-permute-done.10.refs_2_
  89.2 1.3 %collective-permute-start.18 = (bf16[2,128,128]{2,1,0:T(8,128)(2,1)S(1)}, bf16[2,128,128]{2,1,0:T(8,128)(2,1)S(1)}, u32[]{:S(2)}, u32[]{:S(2)}) collective-permute-start(bf16[2,128,128]{2,1,0:T(8,128)(2,1)S(1)} %get-tuple-element.43), channel_id=1, source_target_pairs={{1,6},{3,4},{5,2},{7,0},{9,14},{11,12},{13,10},{15,8},{17,22},{19,... | collective-permute-start | bytes 196616 | tf_op jit(solution)/shard_map/ppermute | solution.py:306
  90.5 0.0 collective-permute-done.11.refs_3_
  90.5 3.7 %collective-permute-done.15.refs_4_ = bf16[2,128,128]{2,1,0:T(8,128)(2,1)S(1)} collective-permute-done((bf16[2,128,128]{2,1,0:T(8,128)(2,1)S(1)}, bf16[2,128,128]{2,1,0:T(8,128)(2,1)S(1)}, u32[]{:S(2)}, u32[]{:S(2)}) %collective-permute-start.15) | collective-permute-done | bytes 65568 | tf_op jit(solution)/shard_map/ppermute | solution.py:306
  94.2 0.3 collective-permute-done.16.refs_5_
  94.4 3.0 %collective-permute-done.17.refs_6_ = bf16[2,128,128]{2,1,0:T(8,128)(2,1)S(1)} collective-permute-done((bf16[2,128,128]{2,1,0:T(8,128)(2,1)S(1)}, bf16[2,128,128]{2,1,0:T(8,128)(2,1)S(1)}, u32[]{:S(2)}, u32[]{:S(2)}) %collective-permute-start.17) | collective-permute-done | bytes 65568 | tf_op jit(solution)/shard_map/ppermute | solution.py:306
  97.4 0.3 collective-permute-done.18.refs_7_
  97.8 0.0 copy-done.5
  97.8 0.3 copy-done.11
  98.0 0.6 copy-done.12
  98.6 2.3 %shard_map.87 = (bf16[1,32,128,128]{3,2,1,0:T(8,128)(2,1)}, bf16[1,4,128,128]{3,2,1,0:T(8,128)(2,1)}, bf16[1,4,128,128]{3,2,1,0:T(8,128)(2,1)}) custom-call(s32[3]{0:T(128)} %copy-done.2, bf16[8,128,128]{2,1,0:T(8,128)(2,1)} %copy-done.3, bf16[8,128,128]{2,1,0:T(8,128)(2,1)} %copy-done.4, bf16[8,128,128]{2,1,0:T(8,128)(2,1)} %copy-done.5, ...), custom_call_target="tpu_custom_call" | custom-call | tf_op jit(solution)/shard_map/pallas_call | solution.py:269
  (24 shorter events, 0.2 us)
Async XLA Ops:
  0.7 2.4 %copy-start.7 = (bf16[1,4,128,128]{3,2,1,0:T(8,128)(2,1)S(1)}, bf16[1,4,128,128]{3,2,1,0:T(8,128)(2,1)}, u32[]{:S(2)}) copy-start(bf16[1,4,128,128]{3,2,1,0:T(8,128)(2,1)} %param.8) | copy-start | bytes 393220
  0.7 2.4 %copy-start.8 = (bf16[1,4,128,128]{3,2,1,0:T(8,128)(2,1)S(1)}, bf16[1,4,128,128]{3,2,1,0:T(8,128)(2,1)}, u32[]{:S(2)}) copy-start(bf16[1,4,128,128]{3,2,1,0:T(8,128)(2,1)} %param.7) | copy-start | bytes 393220
  0.7 2.5 %copy-start = (bf16[1,32,128,128]{3,2,1,0:T(8,128)(2,1)S(1)}, bf16[1,32,128,128]{3,2,1,0:T(8,128)(2,1)}, u32[]{:S(2)}) copy-start(bf16[1,32,128,128]{3,2,1,0:T(8,128)(2,1)} %refs_1_.1) | copy-start | bytes 3145732
  0.7 2.5 %copy-start.1 = (bf16[1,32,128,128]{3,2,1,0:T(8,128)(2,1)S(1)}, bf16[1,32,128,128]{3,2,1,0:T(8,128)(2,1)}, u32[]{:S(2)}) copy-start(bf16[1,32,128,128]{3,2,1,0:T(8,128)(2,1)} %refs_0_.1) | copy-start | bytes 3145732
  3.4 4.7 %collective-permute-start = (bf16[19,128,128]{2,1,0:T(8,128)(2,1)S(1)}, bf16[19,128,128]{2,1,0:T(8,128)(2,1)S(1)}, u32[]{:S(2)}, u32[]{:S(2)}) collective-permute-start(bf16[19,128,128]{2,1,0:T(8,128)(2,1)S(1)} %pad_maximum_fusion), channel_id=1, source_target_pairs={{0,2},{2,0},{4,6},{6,4},{8,10},{10,8},{12,14},{14,12},{16,18},{18,... | collective-permute-start | bytes 1867784 | tf_op jit(solution)/shard_map/ppermute | solution.py:293
  3.5 4.6 %collective-permute-start.2 = (bf16[2,128,128]{2,1,0:T(8,128)(2,1)S(1)}, bf16[2,128,128]{2,1,0:T(8,128)(2,1)S(1)}, u32[]{:S(2)}, u32[]{:S(2)}) collective-permute-start(bf16[2,128,128]{2,1,0:T(8,128)(2,1)S(1)} %pad_maximum_fusion.3), channel_id=1, source_target_pairs={{0,6},{2,4},{4,2},{6,0},{8,14},{10,12},{12,10},{14,8},{16,22},{18,... | collective-permute-start | bytes 196616 | tf_op jit(solution)/shard_map/ppermute | solution.py:293
  5.2 4.7 %collective-permute-start.1 = (bf16[2,128,128]{2,1,0:T(8,128)(2,1)S(1)}, bf16[2,128,128]{2,1,0:T(8,128)(2,1)S(1)}, u32[]{:S(2)}, u32[]{:S(2)}) collective-permute-start(bf16[2,128,128]{2,1,0:T(8,128)(2,1)S(1)} %pad_maximum_fusion.2), channel_id=1, source_target_pairs={{0,4},{2,6},{4,0},{6,2},{8,12},{10,14},{12,8},{14,10},{16,20},{18,... | collective-permute-start | bytes 196616 | tf_op jit(solution)/shard_map/ppermute | solution.py:293
  6.6 41.5 %collective-permute-start.8 = (bf16[17,128,128]{2,1,0:T(8,128)(2,1)}, bf16[17,128,128]{2,1,0:T(8,128)(2,1)}, u32[]{:S(2)}, u32[]{:S(2)}) collective-permute-start(bf16[17,128,128]{2,1,0:T(8,128)(2,1)} %fusion.2), channel_id=1, source_target_pairs={{0,4},{2,6},{4,0},{6,2},{8,12},{10,14},{12,8},{14,10},{16,20},{18,... | collective-permute-start | bytes 1671176 | tf_op jit(solution)/shard_map/ppermute | solution.py:293
  9.9 21.5 %collective-permute-start.3 = (bf16[2,4,128,128]{3,2,1,0:T(8,128)(2,1)S(1)}, bf16[2,4,128,128]{3,2,1,0:T(8,128)(2,1)S(1)}, u32[]{:S(2)}, u32[]{:S(2)}) collective-permute-start(bf16[2,4,128,128]{3,2,1,0:T(8,128)(2,1)S(1)} %pad_maximum_fusion.1.refs_4_), channel_id=1, source_target_pairs={{0,8},{2,10},{4,12},{6,14},{8,16},{10,18},{12,20},{14,22},{16,24},... | collective-permute-start | bytes 786440 | tf_op jit(solution)/shard_map/ppermute | solution.py:298
  13.4 21.2 %collective-permute-start.4 = (bf16[2,4,128,128]{3,2,1,0:T(8,128)(2,1)S(1)}, bf16[2,4,128,128]{3,2,1,0:T(8,128)(2,1)S(1)}, u32[]{:S(2)}, u32[]{:S(2)}) collective-permute-start(bf16[2,4,128,128]{3,2,1,0:T(8,128)(2,1)S(1)} %pad_maximum_fusion.1.refs_4_), channel_id=1, source_target_pairs={{0,16},{2,18},{4,20},{6,22},{8,24},{10,26},{12,28},{14,30},{1,17},... | collective-permute-start | bytes 786440 | tf_op jit(solution)/shard_map/ppermute | solution.py:298
  15.7 18.8 %collective-permute-start.5 = (bf16[2,4,128,128]{3,2,1,0:T(8,128)(2,1)S(1)}, bf16[2,4,128,128]{3,2,1,0:T(8,128)(2,1)}, u32[]{:S(2)}, u32[]{:S(2)}) collective-permute-start(bf16[2,4,128,128]{3,2,1,0:T(8,128)(2,1)S(1)} %pad_maximum_fusion.1.refs_4_), channel_id=1, source_target_pairs={{0,24},{2,26},{4,28},{6,30},{1,25},{3,27},{5,29},{7,31}} | collective-permute-start | bytes 786440 | tf_op jit(solution)/shard_map/ppermute | solution.py:298
  18.0 30.2 %collective-permute-start.9 = (bf16[17,128,128]{2,1,0:T(8,128)(2,1)}, bf16[17,128,128]{2,1,0:T(8,128)(2,1)}, u32[]{:S(2)}, u32[]{:S(2)}) collective-permute-start(bf16[17,128,128]{2,1,0:T(8,128)(2,1)} %fusion.3), channel_id=1, source_target_pairs={{0,6},{2,4},{4,2},{6,0},{8,14},{10,12},{12,10},{14,8},{16,22},{18,... | collective-permute-start | bytes 1671176 | tf_op jit(solution)/shard_map/ppermute | solution.py:293
  18.9 29.2 %copy-start.2 = (s32[3]{0:T(128)}, s32[3]{0:T(128)S(1)}, u32[]{:S(2)}) copy-start(s32[3]{0:T(128)S(1)} %pad_add_fusion.meta) | copy-start | bytes 40
  45.5 17.0 %collective-permute-start.6 = (bf16[8,128,128]{2,1,0:T(8,128)(2,1)S(1)}, bf16[8,128,128]{2,1,0:T(8,128)(2,1)S(1)}, u32[]{:S(2)}, u32[]{:S(2)}) collective-permute-start(bf16[8,128,128]{2,1,0:T(8,128)(2,1)S(1)} %get-tuple-element.20), channel_id=1, source_target_pairs={{1,0},{3,2},{5,4},{7,6},{9,8},{11,10},{13,12},{15,14},{17,16},{19,... | collective-permute-start | bytes 786440 | tf_op jit(solution)/shard_map/ppermute | solution.py:306
  46.8 15.7 %collective-permute-start.7 = (bf16[8,128,128]{2,1,0:T(8,128)(2,1)S(1)}, bf16[8,128,128]{2,1,0:T(8,128)(2,1)S(1)}, u32[]{:S(2)}, u32[]{:S(2)}) collective-permute-start(bf16[8,128,128]{2,1,0:T(8,128)(2,1)S(1)} %get-tuple-element.21), channel_id=1, source_target_pairs={{1,2},{3,0},{5,6},{7,4},{9,10},{11,8},{13,14},{15,12},{17,18},{19,... | collective-permute-start | bytes 786440 | tf_op jit(solution)/shard_map/ppermute | solution.py:306
  62.5 22.7 %copy-start.3 = (bf16[8,128,128]{2,1,0:T(8,128)(2,1)}, bf16[8,128,128]{2,1,0:T(8,128)(2,1)S(1)}, u32[]{:S(2)}) copy-start(bf16[8,128,128]{2,1,0:T(8,128)(2,1)S(1)} %collective-permute-done.6.refs_0_) | copy-start | bytes 786436
  62.5 22.7 %copy-start.4 = (bf16[8,128,128]{2,1,0:T(8,128)(2,1)}, bf16[8,128,128]{2,1,0:T(8,128)(2,1)S(1)}, u32[]{:S(2)}) copy-start(bf16[8,128,128]{2,1,0:T(8,128)(2,1)S(1)} %collective-permute-done.7.refs_1_) | copy-start | bytes 786436
  62.5 6.6 %collective-permute-start.14 = (bf16[2,4,128,128]{3,2,0,1:T(8,128)(2,1)S(1)}, bf16[2,4,128,128]{3,2,0,1:T(8,128)(2,1)S(1)}, u32[]{:S(2)}, u32[]{:S(2)}) collective-permute-start(bf16[2,4,128,128]{3,2,0,1:T(8,128)(2,1)S(1)} %copy.12), channel_id=1, source_target_pairs={{24,0},{26,2},{28,4},{30,6},{25,1},{27,3},{29,5},{31,7}} | collective-permute-start | bytes 786440 | tf_op jit(solution)/shard_map/ppermute | solution.py:298
  63.3 16.6 %collective-permute-start.13 = (bf16[2,4,128,128]{3,2,0,1:T(8,128)(2,1)S(1)}, bf16[2,4,128,128]{3,2,0,1:T(8,128)(2,1)S(1)}, u32[]{:S(2)}, u32[]{:S(2)}) collective-permute-start(bf16[2,4,128,128]{3,2,0,1:T(8,128)(2,1)S(1)} %copy.11), channel_id=1, source_target_pairs={{16,0},{18,2},{20,4},{22,6},{24,8},{26,10},{28,12},{30,14},{17,1},... | collective-permute-start | bytes 786440 | tf_op jit(solution)/shard_map/ppermute | solution.py:298
  64.6 20.5 %collective-permute-start.12 = (bf16[2,4,128,128]{3,2,0,1:T(8,128)(2,1)S(1)}, bf16[2,4,128,128]{3,2,0,1:T(8,128)(2,1)S(1)}, u32[]{:S(2)}, u32[]{:S(2)}) collective-permute-start(bf16[2,4,128,128]{3,2,0,1:T(8,128)(2,1)S(1)} %copy.9), channel_id=1, source_target_pairs={{8,0},{10,2},{12,4},{14,6},{16,8},{18,10},{20,12},{22,14},{24,16},... | collective-permute-start | bytes 786440 | tf_op jit(solution)/shard_map/ppermute | solution.py:298
  66.5 22.7 %collective-permute-start.10 = (bf16[8,128,128]{2,1,0:T(8,128)(2,1)S(1)}, bf16[8,128,128]{2,1,0:T(8,128)(2,1)S(1)}, u32[]{:S(2)}, u32[]{:S(2)}) collective-permute-start(bf16[8,128,128]{2,1,0:T(8,128)(2,1)S(1)} %get-tuple-element.31), channel_id=1, source_target_pairs={{1,4},{3,6},{5,0},{7,2},{9,12},{11,14},{13,8},{15,10},{17,20},{19,... | collective-permute-start | bytes 786440 | tf_op jit(solution)/shard_map/ppermute | solution.py:306
  67.8 22.7 %collective-permute-start.11 = (bf16[8,128,128]{2,1,0:T(8,128)(2,1)S(1)}, bf16[8,128,128]{2,1,0:T(8,128)(2,1)S(1)}, u32[]{:S(2)}, u32[]{:S(2)}) collective-permute-start(bf16[8,128,128]{2,1,0:T(8,128)(2,1)S(1)} %get-tuple-element.32), channel_id=1, source_target_pairs={{1,6},{3,4},{5,2},{7,0},{9,14},{11,12},{13,10},{15,8},{17,22},{19,... | collective-permute-start | bytes 786440 | tf_op jit(solution)/shard_map/ppermute | solution.py:306
  85.3 8.9 %collective-permute-start.15 = (bf16[2,128,128]{2,1,0:T(8,128)(2,1)S(1)}, bf16[2,128,128]{2,1,0:T(8,128)(2,1)S(1)}, u32[]{:S(2)}, u32[]{:S(2)}) collective-permute-start(bf16[2,128,128]{2,1,0:T(8,128)(2,1)S(1)} %get-tuple-element.46), channel_id=1, source_target_pairs={{1,0},{3,2},{5,4},{7,6},{9,8},{11,10},{13,12},{15,14},{17,16},{19,... | collective-permute-start | bytes 196616 | tf_op jit(solution)/shard_map/ppermute | solution.py:306
  86.6 7.9 %collective-permute-start.16 = (bf16[2,128,128]{2,1,0:T(8,128)(2,1)S(1)}, bf16[2,128,128]{2,1,0:T(8,128)(2,1)S(1)}, u32[]{:S(2)}, u32[]{:S(2)}) collective-permute-start(bf16[2,128,128]{2,1,0:T(8,128)(2,1)S(1)} %get-tuple-element.45), channel_id=1, source_target_pairs={{1,2},{3,0},{5,6},{7,4},{9,10},{11,8},{13,14},{15,12},{17,18},{19,... | collective-permute-start | bytes 196616 | tf_op jit(solution)/shard_map/ppermute | solution.py:306
  87.9 9.5 %collective-permute-start.17 = (bf16[2,128,128]{2,1,0:T(8,128)(2,1)S(1)}, bf16[2,128,128]{2,1,0:T(8,128)(2,1)S(1)}, u32[]{:S(2)}, u32[]{:S(2)}) collective-permute-start(bf16[2,128,128]{2,1,0:T(8,128)(2,1)S(1)} %get-tuple-element.44), channel_id=1, source_target_pairs={{1,4},{3,6},{5,0},{7,2},{9,12},{11,14},{13,8},{15,10},{17,20},{19,... | collective-permute-start | bytes 196616 | tf_op jit(solution)/shard_map/ppermute | solution.py:306
  89.2 8.6 %copy-start.5 = (bf16[8,128,128]{2,1,0:T(8,128)(2,1)}, bf16[8,128,128]{2,1,0:T(8,128)(2,1)S(1)}, u32[]{:S(2)}) copy-start(bf16[8,128,128]{2,1,0:T(8,128)(2,1)S(1)} %collective-permute-done.10.refs_2_) | copy-start | bytes 786436
  89.2 8.6 %collective-permute-start.18 = (bf16[2,128,128]{2,1,0:T(8,128)(2,1)S(1)}, bf16[2,128,128]{2,1,0:T(8,128)(2,1)S(1)}, u32[]{:S(2)}, u32[]{:S(2)}) collective-permute-start(bf16[2,128,128]{2,1,0:T(8,128)(2,1)S(1)} %get-tuple-element.43), channel_id=1, source_target_pairs={{1,6},{3,4},{5,2},{7,0},{9,14},{11,12},{13,10},{15,8},{17,22},{19,... | collective-permute-start | bytes 196616 | tf_op jit(solution)/shard_map/ppermute | solution.py:306
  90.5 7.3 %copy-start.6 = (bf16[8,128,128]{2,1,0:T(8,128)(2,1)}, bf16[8,128,128]{2,1,0:T(8,128)(2,1)S(1)}, u32[]{:S(2)}) copy-start(bf16[8,128,128]{2,1,0:T(8,128)(2,1)S(1)} %collective-permute-done.11.refs_3_) | copy-start | bytes 786436
  94.2 3.6 %copy-start.9 = (bf16[2,128,128]{2,1,0:T(8,128)(2,1)}, bf16[2,128,128]{2,1,0:T(8,128)(2,1)S(1)}, u32[]{:S(2)}) copy-start(bf16[2,128,128]{2,1,0:T(8,128)(2,1)S(1)} %collective-permute-done.15.refs_4_) | copy-start | bytes 196612
  94.4 3.3 %copy-start.10 = (bf16[2,128,128]{2,1,0:T(8,128)(2,1)}, bf16[2,128,128]{2,1,0:T(8,128)(2,1)S(1)}, u32[]{:S(2)}) copy-start(bf16[2,128,128]{2,1,0:T(8,128)(2,1)S(1)} %collective-permute-done.16.refs_5_) | copy-start | bytes 196612
  97.4 0.6 copy-start.11
  98.0 0.6 copy-start.12
where the time goes:
time: 102 us; the launch traced here: 101 us
  waiting for transfers between devices  40.6 us (40%)
  Pallas kernels  27.5 us (27%)
  starting transfers between devices  25.2 us (25%)
  other arithmetic  5.28 us (5%)
  between operations  1.3 us (1%)
  local copies, waits for them, and re-layouts  1.18 us (1%)
    ppermute x6, waiting for transfers between devices, along(): return lax.ppermute(tensor, 'seq', route)  31.6 us
    pallas_call x2, Pallas kernels, attend(): pl.pallas_call(functools.partial(attend_kernel, sizes, first), out_shape=...  25.2 us
    ppermute x6, starting transfers between devices, along(): return lax.ppermute(tensor, 'seq', route)  11.1 us
    ppermute x8, starting transfers between devices, previous(): return lax.ppermute(tensor, ('seq', 'pipe'), route)  10.3 us
    ppermute x8, waiting for transfers between devices, previous(): return lax.ppermute(tensor, ('seq', 'pipe'), route)  7.26 us
    ppermute x5, starting transfers between devices, around(): return lax.ppermute(tensor, 'seq', [(i, i ^ hop) for i in range(devices)])  3.8 us
    reduce_sum x1, other arithmetic, on_device(): jnp.sum(out_grads[0].astype(jnp.float32) * outputs[0].astype(jnp.float32)...  2.31 us
    pallas_call x1, Pallas kernels, settle(): pl.pallas_call(functools.partial(settle_kernel, members, heads), out_shap...  2.27 us
  transfers between devices with their start and end apart: 19, of which 9 were waited for; matrix products, arithmetic and copies ran while one was open for 3% of the time, Pallas kernels for 25%

commit v1 on v0

--- a/solution.py
+++ b/solution.py
@@ -9,7 +9,8 @@
 from jax.sharding import PartitionSpec as P
 
 BLK = 512
-TILE_HEADS = 4
+TILE_HEADS = 2
+CHUNK = 256
 FAR = 1e30
 
 
@@ -38,7 +39,7 @@
         query_outs, take = take[:2], take[2:]
         far_outs, own_out, take = take[:reach], take[reach], take[reach + 1 :]
     query_buf, grad_buf, low_buf, delta_buf, pair_buf, key_acc, value_acc, query_done = take[:8]
-    in_sem, pair_sem, out_sem = take[8:11]
+    in_sem, pair_sem, out_sem, even, odd, dprobs_buf, turned = take[8:15]
     mine = meta[0]
     offsets = (meta[1], meta[2])
     lanes = TILE_HEADS * rows
@@ -60,7 +61,7 @@
         return [
             (pack.at[pl.ds(0, heads)], query_buf.at[place]),
             (pack.at[pl.ds(heads, heads)], grad_buf.at[place]),
-            (pack.at[2 * heads, pl.ds(0, 16)], low_buf.at[place]),
+            (pack.at[2 * heads, pl.ds(0, heads)], low_buf.at[place]),
         ]
 
     loads = [(near.at[:, hop], pair_buf.at[2, :, mine ^ hop]) for hop in range(members)]
@@ -96,34 +97,29 @@
 
     steps = heads // TILE_HEADS
     edge_rows = 2 * rows
-
-    def spans_of(half):
-        return ((0, BLK), (1, BLK), (2, (half + 1) * edge_rows))
-
-    def fetch(part, slot, length):
-        return pair_buf[slot, part].reshape(members * rows, feature)[:length]
+    for slot in range(3):
+        turned[slot] = pair_buf[slot, 0].reshape(BLK, feature).T
+
+    def fetch(part, slot, start, size):
+        return pair_buf[slot, part].reshape(BLK, feature)[start : start + size]
 
     def rows_of(buffer, place, step):
         return buffer[place, pl.ds(step * TILE_HEADS, TILE_HEADS)].reshape(lanes, feature)
 
-    def score(half, place, step):
-        query = rows_of(query_buf, place, step)
-        return [nt(fetch(0, slot, length), query) for slot, length in spans_of(half)]
-
-    def soften(half, place, scores):
-        key_ids = lax.broadcasted_iota(jnp.int32, (edge_rows, lanes), 0)
-        row_ids = lax.broadcasted_iota(jnp.int32, (edge_rows, lanes), 1) % rows
-        fixed = half * edge_rows
-        edge = jnp.where(key_ids <= row_ids + place * rows, scores[2][fixed:], -FAR)
-        scores[2] = jnp.concatenate([scores[2][:fixed], edge], axis=0) if half else edge
-        tops = [jnp.max(part, axis=0, keepdims=True) for part in scores]
-        top = jnp.maximum(jnp.maximum(tops[0] - biases[0], tops[1] - biases[1]), tops[2])
-        shifts = [top + biases[0], top + biases[1], top]
-        raws = [jnp.exp2((part - shift) * sharp) for part, shift in zip(scores, shifts)]
-        total = sum(jnp.sum(raw, axis=0, keepdims=True) for raw in raws)
-        return raws, 1.0 / total
-
-    def spread(half, place, step, raws, inverse):
+    def score(half, index, buffer, span, tops):
+        slot, start, size = span
+        place, step = index // steps, index % steps
+        part = nt(fetch(0, slot, start, size), rows_of(query_buf, place, step))
+        if slot == 2 and start + size > half * edge_rows:
+            key_ids = lax.broadcasted_iota(jnp.int32, (size, lanes), 0) + start
+            row_ids = lax.broadcasted_iota(jnp.int32, (size, lanes), 1) % rows
+            part = jnp.where(key_ids <= row_ids + (2 * half + place) * rows, part, -FAR)
+        base = slot * BLK + start
+        buffer[base : base + size] = part
+        tops[slot] = jnp.maximum(tops[slot], jnp.max(part, axis=0, keepdims=True))
+
+    def tile(half, index, tops, now, later):
+        place, step = index // steps, index % steps
         query = rows_of(query_buf, place, step)
         grad = rows_of(grad_buf, place, step)
         delta = jnp.concatenate(
@@ -133,30 +129,59 @@
             ],
             axis=1,
         )
-        query_sum = jnp.zeros((lanes, feature), jnp.float32)
-        for (slot, length), raw in zip(spans_of(half), raws):
-            dprobs = nt(fetch(1, slot, length), grad)
-            probs = raw * inverse
-            dscores = (probs * (dprobs - delta)).astype(jnp.bfloat16)
-            base = slot * BLK
-            value_acc[base : base + length] += nn(probs.astype(jnp.bfloat16), grad)
-            key_acc[base : base + length] += nn(dscores, query)
-            query_sum += tn(dscores, fetch(0, slot, length))
+        spans = spans_of(half)
+        top = jnp.maximum(jnp.maximum(tops[0] - biases[0], tops[1] - biases[1]), tops[2])
+        shifts = [top + biases[0], top + biases[1], top]
+        total = jnp.zeros((1, lanes), jnp.float32)
+        fresh = [jnp.full((1, lanes), -FAR, jnp.float32)] * 3
+        for span in spans:
+            slot, start, size = span
+            base = slot * BLK + start
+            score(half, jnp.minimum(index + 1, 2 * steps - 1), later, span, fresh)
+            dprobs_buf[base : base + size] = nt(fetch(1, slot, start, size), grad)
+            raw = jnp.exp2((now[base : base + size] - shifts[slot]) * sharp)
+            now[base : base + size] = raw
+            total += jnp.sum(raw, axis=0, keepdims=True)
+        inverse = 1.0 / total
+        query_sum = jnp.zeros((feature, lanes), jnp.float32)
+        held = None
+        for span in spans + [None]:
+            if span is not None:
+                slot, start, size = span
+                base = slot * BLK + start
+                probs = now[base : base + size] * inverse
+                dscores = (probs * (dprobs_buf[base : base + size] - delta)).astype(jnp.bfloat16)
+                waiting = (base, size, slot, start, probs.astype(jnp.bfloat16), dscores)
+            if held is not None:
+                base, size, slot, start, probs_low, dscores = held
+                value_acc[base : base + size] += nn(probs_low, grad)
+                key_acc[base : base + size] += nn(dscores, query)
+                query_sum += nn(turned[slot][:, start : start + size], dscores)
+            held = waiting
         query_done[place, pl.ds(step * TILE_HEADS, TILE_HEADS)] = (
-            (query_sum * factor).astype(jnp.bfloat16).reshape(TILE_HEADS, rows, feature)
+            (query_sum.T * factor).astype(jnp.bfloat16).reshape(TILE_HEADS, rows, feature)
         )
+        return fresh
+
+    def spans_of(half):
+        spans = []
+        for slot, length in ((0, BLK), (1, BLK), (2, (half + 1) * edge_rows)):
+            spans += [(slot, start, CHUNK) for start in range(0, length, CHUNK)]
+        return spans
 
     for half in range(members // 2):
 
         @pl.when(group == half)
         def _(half=half):
-            def tile(index, carry, half=half):
-                place, step = index // steps, index % steps
-                raws, inverse = soften(half, place, score(half, place, step))
-                spread(half, place, step, raws, inverse)
-                return carry
-
-            lax.fori_loop(0, 2 * steps, tile, 0)
+            tops = [jnp.full((1, lanes), -FAR, jnp.float32)] * 3
+            for span in spans_of(half):
+                score(half, 0, even, span, tops)
+
+            def body(index, tops):
+                tops = tile(half, 2 * index, list(tops), even, odd)
+                return tuple(tile(half, 2 * index + 1, tops, odd, even))
+
+            lax.fori_loop(0, steps, body, tuple(tops))
 
     stores = [(query_done.at[place], out) for place, out in zip(places, query_outs)]
     if first:
@@ -164,7 +189,7 @@
         for copy in copies:
             copy.wait()
         return
-    far_done, own_done, blank, far_sem = take[11:]
+    far_done, own_done, blank, far_sem = take[15:]
     copies = run(stores, out_sem)
     blank[...] = jnp.zeros_like(blank)
     shape = (members, rows, feature)
@@ -208,8 +233,8 @@
     scratch = [
         pltpu.VMEM((2, heads, rows, feature), low),
         pltpu.VMEM((2, heads, rows, feature), low),
-        pltpu.VMEM((2, 16, rows), low),
-        pltpu.VMEM((2, 16, rows), wide),
+        pltpu.VMEM((2, heads, rows), low),
+        pltpu.VMEM((2, heads, rows), wide),
         pltpu.VMEM((3,) + pair, low),
         pltpu.VMEM(acc, wide),
         pltpu.VMEM(acc, wide),
@@ -217,6 +242,10 @@
         pltpu.SemaphoreType.DMA((members + 8,)),
         pltpu.SemaphoreType.DMA((2,)),
         pltpu.SemaphoreType.DMA((members + 2,)),
+        pltpu.VMEM((3 * BLK, TILE_HEADS * rows), wide),
+        pltpu.VMEM((3 * BLK, TILE_HEADS * rows), wide),
+        pltpu.VMEM((3 * BLK, TILE_HEADS * rows), wide),
+        pltpu.VMEM((3, feature, BLK), low),
     ]
     if first:
         outs += [jax.ShapeDtypeStruct(acc, wide)] * 2
@@ -239,7 +268,7 @@
         cost_estimate=pl.CostEstimate(
             flops=10 * work * feature, transcendentals=work, bytes_accessed=6 * 1024 * 1024
         ),
-        compiler_params=pltpu.CompilerParams(vmem_limit_bytes=48 * 1024 * 1024),
+        compiler_params=pltpu.CompilerParams(vmem_limit_bytes=32 * 1024 * 1024),
     )(meta, *inputs, near, *far)
 
 
@@ -270,9 +299,10 @@
         functools.partial(settle_kernel, members, heads),
         out_shape=[jax.ShapeDtypeStruct(shape, jnp.bfloat16) for shape in shapes],
         in_specs=[pl.BlockSpec(memory_space=pltpu.SMEM)]
-        + [pl.BlockSpec(memory_space=pltpu.VMEM)] * (2 * members),
+        + [anywhere] * (2 * members),
         out_specs=[anywhere] * 3,
         scratch_shapes=[pltpu.SemaphoreType.DMA],
+        compiler_params=pltpu.CompilerParams(vmem_limit_bytes=1024 * 1024),
     )(meta, *query_parts, *pair_parts)
 
 
@@ -284,7 +314,7 @@
     members = BLK // rows
     heads = head_count // key_heads
     reach = devices // members - 1
-    assert members == 4 and key_heads == 4 and heads <= 16
+    assert members == 4 and key_heads == 4 and heads % 8 == 0
     rank = lax.axis_index("seq")
     mine = rank % members
     block = rank // members
@@ -323,14 +353,13 @@
         out_grads[0].astype(jnp.float32) * outputs[0].astype(jnp.float32), axis=-1
     ).astype(jnp.bfloat16)
     deltas = deltas.reshape(key_heads, heads, rows)
-    deltas = jnp.pad(deltas, ((0, 0), (0, 16 - heads), (0, 0)))
 
     def pack_of(hop):
         other = mine ^ hop
         query_part = lax.dynamic_slice_in_dim(queries[0], other * heads, heads, 0)
         grad_part = lax.dynamic_slice_in_dim(out_grads[0], other * heads, heads, 0)
         extra = lax.dynamic_index_in_dim(deltas, other, axis=0, keepdims=True)
-        extra = jnp.pad(extra, ((0, 0), (0, rows - 16), (0, 0)))
+        extra = jnp.pad(extra, ((0, 0), (0, rows - heads), (0, 0)))
         if hop == 1:
             extra = lax.optimization_barrier(jnp.concatenate([extra, pair_of(hop)], axis=0))
         return jnp.concatenate([query_part, grad_part, extra], axis=0)

time: 102 us -> 100 us (0.980)
  Pallas kernels: 27.5 us -> 26 us
where the time goes in v1:
time: 100 us; the launch traced here: 99.3 us
  waiting for transfers between devices  40 us (40%)
  Pallas kernels  26 us (26%)
  starting transfers between devices  25.9 us (26%)
  other arithmetic  5.3 us (5%)
  between operations  1.24 us (1%)
    ppermute x6, waiting for transfers between devices, along(): return lax.ppermute(tensor, 'seq', route)  31.1 us
    pallas_call x2, Pallas kernels, attend(): pl.pallas_call(functools.partial(attend_kernel, sizes, first), out_shape=...  24.4 us
    ppermute x6, starting transfers between devices, along(): return lax.ppermute(tensor, 'seq', route)  11.8 us
    ppermute x8, starting transfers between devices, previous(): return lax.ppermute(tensor, ('seq', 'pipe'), route)  10.3 us
    ppermute x8, waiting for transfers between devices, previous(): return lax.ppermute(tensor, ('seq', 'pipe'), route)  7.13 us
    ppermute x5, starting transfers between devices, around(): return lax.ppermute(tensor, 'seq', [(i, i ^ hop) for i in range(devices)])  3.8 us
    reduce_sum x1, other arithmetic, on_device(): jnp.sum(out_grads[0].astype(jnp.float32) * outputs[0].astype(jnp.float32)...  2.31 us
  transfers between devices with their start and end apart: 19, of which 9 were waited for; matrix products, arithmetic and copies ran while one was open for 3% of the time, Pallas kernels for 25%

profile of v1, /device:TPU:8, one launch (start us, length us, event | category | flops | bytes accessed | tf_op | source)
XLA Modules:
  0.0 99.3 jit_solution(18243299462918934304)
XLA Ops:
  0.7 0.0 copy-start.4
  0.7 0.0 copy-start.5
  0.7 0.0 copy-start
  0.7 0.0 copy-start.1
  0.7 2.3 %multiply_reduce_fusion = bf16[32,128]{1,0:T(8,128)(2,1)S(1)} fusion(bf16[1,32,128,128]{3,2,1,0:T(8,128)(2,1)} %param.9, bf16[1,32,128,128]{3,2,1,0:T(8,128)(2,1)} %refs_1_.1), kind=kLoop, calls=%fused_computation | loop fusion | flops 2093056 | bytes 2105344 | tf_op jit(solution)/shard_map/reduce_sum | solution.py:352
  3.1 0.0 copy-done.4
  3.1 0.0 copy-done.5
  3.1 0.7 dynamic-slice_bitcast_fusion.10
  3.8 0.0 copy-done
  3.8 0.0 copy-done.1
  3.8 0.1 dynamic-slice_bitcast_fusion
  3.9 0.0 copy-start.2
  3.9 0.0 copy-start.3
  4.0 0.1 pad_maximum_fusion
  4.0 0.1 collective-permute-start
  4.1 1.6 %collective-permute-start.2 = (bf16[2,128,128]{2,1,0:T(8,128)(2,1)S(1)}, bf16[2,128,128]{2,1,0:T(8,128)(2,1)S(1)}, u32[]{:S(2)}, u32[]{:S(2)}) collective-permute-start(bf16[2,128,128]{2,1,0:T(8,128)(2,1)S(1)} %pad_maximum_fusion.3), channel_id=1, source_target_pairs={{0,6},{2,4},{4,2},{6,0},{8,14},{10,12},{12,10},{14,8},{16,22},{18,... | collective-permute-start | bytes 196616 | tf_op jit(solution)/shard_map/ppermute | solution.py:323
  5.8 0.6 collective-permute-start.1
  6.4 0.9 fusion.2
  7.3 1.5 %collective-permute-start.8 = (bf16[17,128,128]{2,1,0:T(8,128)(2,1)}, bf16[17,128,128]{2,1,0:T(8,128)(2,1)S(1)}, u32[]{:S(2)}, u32[]{:S(2)}) collective-permute-start(bf16[17,128,128]{2,1,0:T(8,128)(2,1)} %fusion.2), channel_id=1, source_target_pairs={{0,4},{2,6},{4,0},{6,2},{8,12},{10,14},{12,8},{14,10},{16,20},{18,... | collective-permute-start | bytes 1671176 | tf_op jit(solution)/shard_map/ppermute | solution.py:323
  8.8 0.0 copy-done.2
  8.8 0.0 copy-done.3
  8.8 0.0 collective-permute-done.refs_3_
  8.8 0.0 collective-permute-done.2
  8.8 1.7 %collective-permute-done.1 = bf16[2,128,128]{2,1,0:T(8,128)(2,1)S(1)} collective-permute-done((bf16[2,128,128]{2,1,0:T(8,128)(2,1)S(1)}, bf16[2,128,128]{2,1,0:T(8,128)(2,1)S(1)}, u32[]{:S(2)}, u32[]{:S(2)}) %collective-permute-start.1) | collective-permute-done | bytes 65568 | tf_op jit(solution)/shard_map/ppermute | solution.py:323
  10.5 3.5 %collective-permute-start.3 = (bf16[2,4,128,128]{3,2,1,0:T(8,128)(2,1)S(1)}, bf16[2,4,128,128]{3,2,1,0:T(8,128)(2,1)}, u32[]{:S(2)}, u32[]{:S(2)}) collective-permute-start(bf16[2,4,128,128]{3,2,1,0:T(8,128)(2,1)S(1)} %pad_maximum_fusion.1.refs_4_), channel_id=1, source_target_pairs={{0,8},{2,10},{4,12},{6,14},{8,16},{10,18},{12,20},{14,22},{16,24},... | collective-permute-start | bytes 786440 | tf_op jit(solution)/shard_map/ppermute | solution.py:328
  14.0 3.0 %collective-permute-start.4 = (bf16[2,4,128,128]{3,2,1,0:T(8,128)(2,1)S(1)}, bf16[2,4,128,128]{3,2,1,0:T(8,128)(2,1)}, u32[]{:S(2)}, u32[]{:S(2)}) collective-permute-start(bf16[2,4,128,128]{3,2,1,0:T(8,128)(2,1)S(1)} %pad_maximum_fusion.1.refs_4_), channel_id=1, source_target_pairs={{0,16},{2,18},{4,20},{6,22},{8,24},{10,26},{12,28},{14,30},{1,17},... | collective-permute-start | bytes 786440 | tf_op jit(solution)/shard_map/ppermute | solution.py:328
  17.1 1.4 %collective-permute-start.5 = (bf16[2,4,128,128]{3,2,1,0:T(8,128)(2,1)S(1)}, bf16[2,4,128,128]{3,2,1,0:T(8,128)(2,1)}, u32[]{:S(2)}, u32[]{:S(2)}) collective-permute-start(bf16[2,4,128,128]{3,2,1,0:T(8,128)(2,1)S(1)} %pad_maximum_fusion.1.refs_4_), channel_id=1, source_target_pairs={{0,24},{2,26},{4,28},{6,30},{1,25},{3,27},{5,29},{7,31}} | collective-permute-start | bytes 786440 | tf_op jit(solution)/shard_map/ppermute | solution.py:328
  18.4 0.9 fusion.3
  19.3 0.0 collective-permute-start.9
  19.3 0.9 fusion.10
  20.2 0.1 pad_add_fusion.meta
  20.3 11.7 %collective-permute-done.3.refs_5_ = bf16[2,4,128,128]{3,2,1,0:T(8,128)(2,1)} collective-permute-done((bf16[2,4,128,128]{3,2,1,0:T(8,128)(2,1)S(1)}, bf16[2,4,128,128]{3,2,1,0:T(8,128)(2,1)}, u32[]{:S(2)}, u32[]{:S(2)}) %collective-permute-start.3) | collective-permute-done | bytes 262176 | tf_op jit(solution)/shard_map/ppermute | solution.py:328
  32.0 3.2 %collective-permute-done.4.refs_6_ = bf16[2,4,128,128]{3,2,1,0:T(8,128)(2,1)} collective-permute-done((bf16[2,4,128,128]{3,2,1,0:T(8,128)(2,1)S(1)}, bf16[2,4,128,128]{3,2,1,0:T(8,128)(2,1)}, u32[]{:S(2)}, u32[]{:S(2)}) %collective-permute-start.4) | collective-permute-done | bytes 262176 | tf_op jit(solution)/shard_map/ppermute | solution.py:328
  35.2 0.0 collective-permute-done.5.refs_7_
  35.2 11.1 %shard_map.85 = (bf16[8,128,128]{2,1,0:T(8,128)(2,1)S(1)}, bf16[8,128,128]{2,1,0:T(8,128)(2,1)S(1)}, f32[1536,128]{1,0:T(8,128)S(1)}, f32[1536,128]{1,0:T(8,128)S(1)}) custom-call(s32[3]{0:T(128)S(1)} %pad_add_fusion.meta, bf16[1,32,128,128]{3,2,1,0:T(8,128)(2,1)S(1)} %copy-done.1, bf16[1,32,128,128]{3,2,1,0:T(8,128)(2,1)S(1)} %copy-done, ...), custom_call_target="tpu_custom_call" | custom-call | flops 3690987520 | bytes 6291456 | tf_op jit(solution)/shard_map/pallas_call | solution.py:261
  46.3 1.3 %collective-permute-start.6 = (bf16[8,128,128]{2,1,0:T(8,128)(2,1)S(1)}, bf16[8,128,128]{2,1,0:T(8,128)(2,1)S(1)}, u32[]{:S(2)}, u32[]{:S(2)}) collective-permute-start(bf16[8,128,128]{2,1,0:T(8,128)(2,1)S(1)} %get-tuple-element.20), channel_id=1, source_target_pairs={{1,0},{3,2},{5,4},{7,6},{9,8},{11,10},{13,12},{15,14},{17,16},{19,... | collective-permute-start | bytes 786440 | tf_op jit(solution)/shard_map/ppermute | solution.py:336
  47.6 1.3 %collective-permute-start.7 = (bf16[8,128,128]{2,1,0:T(8,128)(2,1)S(1)}, bf16[8,128,128]{2,1,0:T(8,128)(2,1)S(1)}, u32[]{:S(2)}, u32[]{:S(2)}) collective-permute-start(bf16[8,128,128]{2,1,0:T(8,128)(2,1)S(1)} %get-tuple-element.21), channel_id=1, source_target_pairs={{1,2},{3,0},{5,6},{7,4},{9,10},{11,8},{13,14},{15,12},{17,18},{19,... | collective-permute-start | bytes 786440 | tf_op jit(solution)/shard_map/ppermute | solution.py:336
  48.9 0.0 collective-permute-done.8.refs_0_
  48.9 0.0 collective-permute-done.9.refs_1_
  48.9 13.3 %shard_map.86 = (bf16[8,128,128]{2,1,0:T(8,128)(2,1)S(1)}, bf16[8,128,128]{2,1,0:T(8,128)(2,1)S(1)}, bf16[2,4,128,128]{3,2,1,0:T(8,128)(2,1)S(1)}, bf16[2,4,128,...) custom-call(s32[3]{0:T(128)S(1)} %pad_add_fusion.meta, ...), custom_call_target="tpu_custom_call" | custom-call | flops 3690987520 | bytes 6291456 | tf_op jit(solution)/shard_map/pallas_call | solution.py:261
  62.2 0.0 collective-permute-done.6.refs_0_
  62.3 0.0 collective-permute-done.7.refs_1_
  62.3 0.7 collective-permute-start.14
  63.0 1.3 %collective-permute-start.13 = (bf16[2,4,128,128]{3,2,0,1:T(8,128)(2,1)S(1)}, bf16[2,4,128,128]{3,2,0,1:T(8,128)(2,1)S(1)}, u32[]{:S(2)}, u32[]{:S(2)}) collective-permute-start(bf16[2,4,128,128]{3,2,0,1:T(8,128)(2,1)S(1)} %copy.11), channel_id=1, source_target_pairs={{16,0},{18,2},{20,4},{22,6},{24,8},{26,10},{28,12},{30,14},{17,1},... | collective-permute-start | bytes 786440 | tf_op jit(solution)/shard_map/ppermute | solution.py:328
  64.3 1.9 %collective-permute-start.12 = (bf16[2,4,128,128]{3,2,0,1:T(8,128)(2,1)S(1)}, bf16[2,4,128,128]{3,2,0,1:T(8,128)(2,1)S(1)}, u32[]{:S(2)}, u32[]{:S(2)}) collective-permute-start(bf16[2,4,128,128]{3,2,0,1:T(8,128)(2,1)S(1)} %copy.9), channel_id=1, source_target_pairs={{8,0},{10,2},{12,4},{14,6},{16,8},{18,10},{20,12},{22,14},{24,16},... | collective-permute-start | bytes 786440 | tf_op jit(solution)/shard_map/ppermute | solution.py:328
  66.3 1.3 %collective-permute-start.10 = (bf16[8,128,128]{2,1,0:T(8,128)(2,1)S(1)}, bf16[8,128,128]{2,1,0:T(8,128)(2,1)S(1)}, u32[]{:S(2)}, u32[]{:S(2)}) collective-permute-start(bf16[8,128,128]{2,1,0:T(8,128)(2,1)S(1)} %get-tuple-element.31), channel_id=1, source_target_pairs={{1,4},{3,6},{5,0},{7,2},{9,12},{11,14},{13,8},{15,10},{17,20},{19,... | collective-permute-start | bytes 786440 | tf_op jit(solution)/shard_map/ppermute | solution.py:336
  67.6 1.3 %collective-permute-start.11 = (bf16[8,128,128]{2,1,0:T(8,128)(2,1)S(1)}, bf16[8,128,128]{2,1,0:T(8,128)(2,1)S(1)}, u32[]{:S(2)}, u32[]{:S(2)}) collective-permute-start(bf16[8,128,128]{2,1,0:T(8,128)(2,1)S(1)} %get-tuple-element.32), channel_id=1, source_target_pairs={{1,6},{3,4},{5,2},{7,0},{9,14},{11,12},{13,10},{15,8},{17,22},{19,... | collective-permute-start | bytes 786440 | tf_op jit(solution)/shard_map/ppermute | solution.py:336
  68.9 0.0 collective-permute-done.14
  68.9 11.0 %collective-permute-done.13 = bf16[2,4,128,128]{3,2,0,1:T(8,128)(2,1)S(1)} collective-permute-done((bf16[2,4,128,128]{3,2,0,1:T(8,128)(2,1)S(1)}, bf16[2,4,128,128]{3,2,0,1:T(8,128)(2,1)S(1)}, u32[]{:S(2)}, u32[]{:S(2)}) %collective-permute-start.13) | collective-permute-done | bytes 262176 | tf_op jit(solution)/shard_map/ppermute | solution.py:328
  79.9 5.2 %collective-permute-done.12 = bf16[2,4,128,128]{3,2,0,1:T(8,128)(2,1)S(1)} collective-permute-done((bf16[2,4,128,128]{3,2,0,1:T(8,128)(2,1)S(1)}, bf16[2,4,128,128]{3,2,0,1:T(8,128)(2,1)S(1)}, u32[]{:S(2)}, u32[]{:S(2)}) %collective-permute-start.12) | collective-permute-done | bytes 262176 | tf_op jit(solution)/shard_map/ppermute | solution.py:328
  85.1 0.1 fusion.6
  85.2 1.3 %collective-permute-start.15 = (bf16[2,128,128]{2,1,0:T(8,128)(2,1)S(1)}, bf16[2,128,128]{2,1,0:T(8,128)(2,1)S(1)}, u32[]{:S(2)}, u32[]{:S(2)}) collective-permute-start(bf16[2,128,128]{2,1,0:T(8,128)(2,1)S(1)} %get-tuple-element.46), channel_id=1, source_target_pairs={{1,0},{3,2},{5,4},{7,6},{9,8},{11,10},{13,12},{15,14},{17,16},{19,... | collective-permute-start | bytes 196616 | tf_op jit(solution)/shard_map/ppermute | solution.py:336
  86.5 1.3 %collective-permute-start.16 = (bf16[2,128,128]{2,1,0:T(8,128)(2,1)S(1)}, bf16[2,128,128]{2,1,0:T(8,128)(2,1)S(1)}, u32[]{:S(2)}, u32[]{:S(2)}) collective-permute-start(bf16[2,128,128]{2,1,0:T(8,128)(2,1)S(1)} %get-tuple-element.45), channel_id=1, source_target_pairs={{1,2},{3,0},{5,6},{7,4},{9,10},{11,8},{13,14},{15,12},{17,18},{19,... | collective-permute-start | bytes 196616 | tf_op jit(solution)/shard_map/ppermute | solution.py:336
  87.8 1.3 %collective-permute-start.17 = (bf16[2,128,128]{2,1,0:T(8,128)(2,1)S(1)}, bf16[2,128,128]{2,1,0:T(8,128)(2,1)S(1)}, u32[]{:S(2)}, u32[]{:S(2)}) collective-permute-start(bf16[2,128,128]{2,1,0:T(8,128)(2,1)S(1)} %get-tuple-element.44), channel_id=1, source_target_pairs={{1,4},{3,6},{5,0},{7,2},{9,12},{11,14},{13,8},{15,10},{17,20},{19,... | collective-permute-start | bytes 196616 | tf_op jit(solution)/shard_map/ppermute | solution.py:336
  89.1 0.0 collective-permute-done.10.refs_2_
  89.1 1.3 %collective-permute-start.18 = (bf16[2,128,128]{2,1,0:T(8,128)(2,1)S(1)}, bf16[2,128,128]{2,1,0:T(8,128)(2,1)S(1)}, u32[]{:S(2)}, u32[]{:S(2)}) collective-permute-start(bf16[2,128,128]{2,1,0:T(8,128)(2,1)S(1)} %get-tuple-element.43), channel_id=1, source_target_pairs={{1,6},{3,4},{5,2},{7,0},{9,14},{11,12},{13,10},{15,8},{17,22},{19,... | collective-permute-start | bytes 196616 | tf_op jit(solution)/shard_map/ppermute | solution.py:336
  90.4 0.0 collective-permute-done.11.refs_3_
  90.4 3.7 %collective-permute-done.15.refs_4_ = bf16[2,128,128]{2,1,0:T(8,128)(2,1)S(1)} collective-permute-done((bf16[2,128,128]{2,1,0:T(8,128)(2,1)S(1)}, bf16[2,128,128]{2,1,0:T(8,128)(2,1)S(1)}, u32[]{:S(2)}, u32[]{:S(2)}) %collective-permute-start.15) | collective-permute-done | bytes 65568 | tf_op jit(solution)/shard_map/ppermute | solution.py:336
  94.1 0.3 collective-permute-done.16.refs_5_
  94.4 2.9 %collective-permute-done.17.refs_6_ = bf16[2,128,128]{2,1,0:T(8,128)(2,1)S(1)} collective-permute-done((bf16[2,128,128]{2,1,0:T(8,128)(2,1)S(1)}, bf16[2,128,128]{2,1,0:T(8,128)(2,1)S(1)}, u32[]{:S(2)}, u32[]{:S(2)}) %collective-permute-start.17) | collective-permute-done | bytes 65568 | tf_op jit(solution)/shard_map/ppermute | solution.py:336
  97.3 0.3 collective-permute-done.18.refs_7_
  97.6 1.6 %shard_map.87 = (bf16[1,32,128,128]{3,2,1,0:T(8,128)(2,1)}, bf16[1,4,128,128]{3,2,1,0:T(8,128)(2,1)}, bf16[1,4,128,128]{3,2,1,0:T(8,128)(2,1)}) custom-call(s32[3]{0:T(128)S(1)} %pad_add_fusion.meta, bf16[8,128,128]{2,1,0:T(8,128)(2,1)S(1)} %collective-permute-done.6.refs_0_, bf16[8,128,128]{2,1,0:T(8,128)(2,1)S(1)} %collective-permute-done.7.refs_1_, ...), custom_call_target="tpu_custom_call" | custom-call | tf_op jit(solution)/shard_map/pallas_call | solution.py:298
  (11 shorter events, 0.2 us)
Async XLA Ops:
  0.7 2.4 %copy-start.4 = (bf16[1,4,128,128]{3,2,1,0:T(8,128)(2,1)S(1)}, bf16[1,4,128,128]{3,2,1,0:T(8,128)(2,1)}, u32[]{:S(2)}) copy-start(bf16[1,4,128,128]{3,2,1,0:T(8,128)(2,1)} %param.8) | copy-start | bytes 393220
  0.7 2.4 %copy-start.5 = (bf16[1,4,128,128]{3,2,1,0:T(8,128)(2,1)S(1)}, bf16[1,4,128,128]{3,2,1,0:T(8,128)(2,1)}, u32[]{:S(2)}) copy-start(bf16[1,4,128,128]{3,2,1,0:T(8,128)(2,1)} %param.7) | copy-start | bytes 393220
  0.7 3.1 %copy-start = (bf16[1,32,128,128]{3,2,1,0:T(8,128)(2,1)S(1)}, bf16[1,32,128,128]{3,2,1,0:T(8,128)(2,1)}, u32[]{:S(2)}) copy-start(bf16[1,32,128,128]{3,2,1,0:T(8,128)(2,1)} %refs_1_.1) | copy-start | bytes 3145732
  0.7 3.1 %copy-start.1 = (bf16[1,32,128,128]{3,2,1,0:T(8,128)(2,1)S(1)}, bf16[1,32,128,128]{3,2,1,0:T(8,128)(2,1)}, u32[]{:S(2)}) copy-start(bf16[1,32,128,128]{3,2,1,0:T(8,128)(2,1)} %refs_0_.1) | copy-start | bytes 3145732
  3.9 4.8 %copy-start.2 = (bf16[1,128,128]{2,1,0:T(8,128)(2,1)S(1)}, bf16[1,128,128]{2,1,0:T(8,128)(2,1)}, u32[]{:S(2)}) copy-start(bf16[1,128,128]{2,1,0:T(8,128)(2,1)} %get-tuple-element.51) | copy-start | bytes 98308
  3.9 4.8 %copy-start.3 = (bf16[1,128,128]{2,1,0:T(8,128)(2,1)S(1)}, bf16[1,128,128]{2,1,0:T(8,128)(2,1)}, u32[]{:S(2)}) copy-start(bf16[1,128,128]{2,1,0:T(8,128)(2,1)} %get-tuple-element.61) | copy-start | bytes 98308
  4.0 4.7 %collective-permute-start = (bf16[19,128,128]{2,1,0:T(8,128)(2,1)S(1)}, bf16[19,128,128]{2,1,0:T(8,128)(2,1)S(1)}, u32[]{:S(2)}, u32[]{:S(2)}) collective-permute-start(bf16[19,128,128]{2,1,0:T(8,128)(2,1)S(1)} %pad_maximum_fusion), channel_id=1, source_target_pairs={{0,2},{2,0},{4,6},{6,4},{8,10},{10,8},{12,14},{14,12},{16,18},{18,... | collective-permute-start | bytes 1867784 | tf_op jit(solution)/shard_map/ppermute | solution.py:323
  4.1 4.7 %collective-permute-start.2 = (bf16[2,128,128]{2,1,0:T(8,128)(2,1)S(1)}, bf16[2,128,128]{2,1,0:T(8,128)(2,1)S(1)}, u32[]{:S(2)}, u32[]{:S(2)}) collective-permute-start(bf16[2,128,128]{2,1,0:T(8,128)(2,1)S(1)} %pad_maximum_fusion.3), channel_id=1, source_target_pairs={{0,6},{2,4},{4,2},{6,0},{8,14},{10,12},{12,10},{14,8},{16,22},{18,... | collective-permute-start | bytes 196616 | tf_op jit(solution)/shard_map/ppermute | solution.py:323
  5.8 4.7 %collective-permute-start.1 = (bf16[2,128,128]{2,1,0:T(8,128)(2,1)S(1)}, bf16[2,128,128]{2,1,0:T(8,128)(2,1)S(1)}, u32[]{:S(2)}, u32[]{:S(2)}) collective-permute-start(bf16[2,128,128]{2,1,0:T(8,128)(2,1)S(1)} %pad_maximum_fusion.2), channel_id=1, source_target_pairs={{0,4},{2,6},{4,0},{6,2},{8,12},{10,14},{12,8},{14,10},{16,20},{18,... | collective-permute-start | bytes 196616 | tf_op jit(solution)/shard_map/ppermute | solution.py:323
  7.3 41.7 %collective-permute-start.8 = (bf16[17,128,128]{2,1,0:T(8,128)(2,1)}, bf16[17,128,128]{2,1,0:T(8,128)(2,1)S(1)}, u32[]{:S(2)}, u32[]{:S(2)}) collective-permute-start(bf16[17,128,128]{2,1,0:T(8,128)(2,1)} %fusion.2), channel_id=1, source_target_pairs={{0,4},{2,6},{4,0},{6,2},{8,12},{10,14},{12,8},{14,10},{16,20},{18,... | collective-permute-start | bytes 1671176 | tf_op jit(solution)/shard_map/ppermute | solution.py:323
  10.5 21.5 %collective-permute-start.3 = (bf16[2,4,128,128]{3,2,1,0:T(8,128)(2,1)S(1)}, bf16[2,4,128,128]{3,2,1,0:T(8,128)(2,1)}, u32[]{:S(2)}, u32[]{:S(2)}) collective-permute-start(bf16[2,4,128,128]{3,2,1,0:T(8,128)(2,1)S(1)} %pad_maximum_fusion.1.refs_4_), channel_id=1, source_target_pairs={{0,8},{2,10},{4,12},{6,14},{8,16},{10,18},{12,20},{14,22},{16,24},... | collective-permute-start | bytes 786440 | tf_op jit(solution)/shard_map/ppermute | solution.py:328
  14.0 21.2 %collective-permute-start.4 = (bf16[2,4,128,128]{3,2,1,0:T(8,128)(2,1)S(1)}, bf16[2,4,128,128]{3,2,1,0:T(8,128)(2,1)}, u32[]{:S(2)}, u32[]{:S(2)}) collective-permute-start(bf16[2,4,128,128]{3,2,1,0:T(8,128)(2,1)S(1)} %pad_maximum_fusion.1.refs_4_), channel_id=1, source_target_pairs={{0,16},{2,18},{4,20},{6,22},{8,24},{10,26},{12,28},{14,30},{1,17},... | collective-permute-start | bytes 786440 | tf_op jit(solution)/shard_map/ppermute | solution.py:328
  17.1 18.2 %collective-permute-start.5 = (bf16[2,4,128,128]{3,2,1,0:T(8,128)(2,1)S(1)}, bf16[2,4,128,128]{3,2,1,0:T(8,128)(2,1)}, u32[]{:S(2)}, u32[]{:S(2)}) collective-permute-start(bf16[2,4,128,128]{3,2,1,0:T(8,128)(2,1)S(1)} %pad_maximum_fusion.1.refs_4_), channel_id=1, source_target_pairs={{0,24},{2,26},{4,28},{6,30},{1,25},{3,27},{5,29},{7,31}} | collective-permute-start | bytes 786440 | tf_op jit(solution)/shard_map/ppermute | solution.py:328
  19.3 29.6 %collective-permute-start.9 = (bf16[17,128,128]{2,1,0:T(8,128)(2,1)}, bf16[17,128,128]{2,1,0:T(8,128)(2,1)}, u32[]{:S(2)}, u32[]{:S(2)}) collective-permute-start(bf16[17,128,128]{2,1,0:T(8,128)(2,1)} %fusion.3), channel_id=1, source_target_pairs={{0,6},{2,4},{4,2},{6,0},{8,14},{10,12},{12,10},{14,8},{16,22},{18,... | collective-permute-start | bytes 1671176 | tf_op jit(solution)/shard_map/ppermute | solution.py:323
  46.3 15.9 %collective-permute-start.6 = (bf16[8,128,128]{2,1,0:T(8,128)(2,1)S(1)}, bf16[8,128,128]{2,1,0:T(8,128)(2,1)S(1)}, u32[]{:S(2)}, u32[]{:S(2)}) collective-permute-start(bf16[8,128,128]{2,1,0:T(8,128)(2,1)S(1)} %get-tuple-element.20), channel_id=1, source_target_pairs={{1,0},{3,2},{5,4},{7,6},{9,8},{11,10},{13,12},{15,14},{17,16},{19,... | collective-permute-start | bytes 786440 | tf_op jit(solution)/shard_map/ppermute | solution.py:336
  47.6 14.6 %collective-permute-start.7 = (bf16[8,128,128]{2,1,0:T(8,128)(2,1)S(1)}, bf16[8,128,128]{2,1,0:T(8,128)(2,1)S(1)}, u32[]{:S(2)}, u32[]{:S(2)}) collective-permute-start(bf16[8,128,128]{2,1,0:T(8,128)(2,1)S(1)} %get-tuple-element.21), channel_id=1, source_target_pairs={{1,2},{3,0},{5,6},{7,4},{9,10},{11,8},{13,14},{15,12},{17,18},{19,... | collective-permute-start | bytes 786440 | tf_op jit(solution)/shard_map/ppermute | solution.py:336
  62.3 6.6 %collective-permute-start.14 = (bf16[2,4,128,128]{3,2,0,1:T(8,128)(2,1)S(1)}, bf16[2,4,128,128]{3,2,0,1:T(8,128)(2,1)S(1)}, u32[]{:S(2)}, u32[]{:S(2)}) collective-permute-start(bf16[2,4,128,128]{3,2,0,1:T(8,128)(2,1)S(1)} %copy.12), channel_id=1, source_target_pairs={{24,0},{26,2},{28,4},{30,6},{25,1},{27,3},{29,5},{31,7}} | collective-permute-start | bytes 786440 | tf_op jit(solution)/shard_map/ppermute | solution.py:328
  63.0 16.9 %collective-permute-start.13 = (bf16[2,4,128,128]{3,2,0,1:T(8,128)(2,1)S(1)}, bf16[2,4,128,128]{3,2,0,1:T(8,128)(2,1)S(1)}, u32[]{:S(2)}, u32[]{:S(2)}) collective-permute-start(bf16[2,4,128,128]{3,2,0,1:T(8,128)(2,1)S(1)} %copy.11), channel_id=1, source_target_pairs={{16,0},{18,2},{20,4},{22,6},{24,8},{26,10},{28,12},{30,14},{17,1},... | collective-permute-start | bytes 786440 | tf_op jit(solution)/shard_map/ppermute | solution.py:328
  64.3 20.7 %collective-permute-start.12 = (bf16[2,4,128,128]{3,2,0,1:T(8,128)(2,1)S(1)}, bf16[2,4,128,128]{3,2,0,1:T(8,128)(2,1)S(1)}, u32[]{:S(2)}, u32[]{:S(2)}) collective-permute-start(bf16[2,4,128,128]{3,2,0,1:T(8,128)(2,1)S(1)} %copy.9), channel_id=1, source_target_pairs={{8,0},{10,2},{12,4},{14,6},{16,8},{18,10},{20,12},{22,14},{24,16},... | collective-permute-start | bytes 786440 | tf_op jit(solution)/shard_map/ppermute | solution.py:328
  66.3 22.9 %collective-permute-start.10 = (bf16[8,128,128]{2,1,0:T(8,128)(2,1)S(1)}, bf16[8,128,128]{2,1,0:T(8,128)(2,1)S(1)}, u32[]{:S(2)}, u32[]{:S(2)}) collective-permute-start(bf16[8,128,128]{2,1,0:T(8,128)(2,1)S(1)} %get-tuple-element.31), channel_id=1, source_target_pairs={{1,4},{3,6},{5,0},{7,2},{9,12},{11,14},{13,8},{15,10},{17,20},{19,... | collective-permute-start | bytes 786440 | tf_op jit(solution)/shard_map/ppermute | solution.py:336
  67.6 22.9 %collective-permute-start.11 = (bf16[8,128,128]{2,1,0:T(8,128)(2,1)S(1)}, bf16[8,128,128]{2,1,0:T(8,128)(2,1)S(1)}, u32[]{:S(2)}, u32[]{:S(2)}) collective-permute-start(bf16[8,128,128]{2,1,0:T(8,128)(2,1)S(1)} %get-tuple-element.32), channel_id=1, source_target_pairs={{1,6},{3,4},{5,2},{7,0},{9,14},{11,12},{13,10},{15,8},{17,22},{19,... | collective-permute-start | bytes 786440 | tf_op jit(solution)/shard_map/ppermute | solution.py:336
  85.2 8.9 %collective-permute-start.15 = (bf16[2,128,128]{2,1,0:T(8,128)(2,1)S(1)}, bf16[2,128,128]{2,1,0:T(8,128)(2,1)S(1)}, u32[]{:S(2)}, u32[]{:S(2)}) collective-permute-start(bf16[2,128,128]{2,1,0:T(8,128)(2,1)S(1)} %get-tuple-element.46), channel_id=1, source_target_pairs={{1,0},{3,2},{5,4},{7,6},{9,8},{11,10},{13,12},{15,14},{17,16},{19,... | collective-permute-start | bytes 196616 | tf_op jit(solution)/shard_map/ppermute | solution.py:336
  86.5 7.9 %collective-permute-start.16 = (bf16[2,128,128]{2,1,0:T(8,128)(2,1)S(1)}, bf16[2,128,128]{2,1,0:T(8,128)(2,1)S(1)}, u32[]{:S(2)}, u32[]{:S(2)}) collective-permute-start(bf16[2,128,128]{2,1,0:T(8,128)(2,1)S(1)} %get-tuple-element.45), channel_id=1, source_target_pairs={{1,2},{3,0},{5,6},{7,4},{9,10},{11,8},{13,14},{15,12},{17,18},{19,... | collective-permute-start | bytes 196616 | tf_op jit(solution)/shard_map/ppermute | solution.py:336
  87.8 9.5 %collective-permute-start.17 = (bf16[2,128,128]{2,1,0:T(8,128)(2,1)S(1)}, bf16[2,128,128]{2,1,0:T(8,128)(2,1)S(1)}, u32[]{:S(2)}, u32[]{:S(2)}) collective-permute-start(bf16[2,128,128]{2,1,0:T(8,128)(2,1)S(1)} %get-tuple-element.44), channel_id=1, source_target_pairs={{1,4},{3,6},{5,0},{7,2},{9,12},{11,14},{13,8},{15,10},{17,20},{19,... | collective-permute-start | bytes 196616 | tf_op jit(solution)/shard_map/ppermute | solution.py:336
  89.1 8.4 %collective-permute-start.18 = (bf16[2,128,128]{2,1,0:T(8,128)(2,1)S(1)}, bf16[2,128,128]{2,1,0:T(8,128)(2,1)S(1)}, u32[]{:S(2)}, u32[]{:S(2)}) collective-permute-start(bf16[2,128,128]{2,1,0:T(8,128)(2,1)S(1)} %get-tuple-element.43), channel_id=1, source_target_pairs={{1,6},{3,4},{5,2},{7,0},{9,14},{11,12},{13,10},{15,8},{17,22},{19,... | collective-permute-start | bytes 196616 | tf_op jit(solution)/shard_map/ppermute | solution.py:336

commit v2 on v1

--- a/solution.py
+++ b/solution.py
@@ -10,7 +10,7 @@
 
 BLK = 512
 TILE_HEADS = 2
-CHUNK = 256
+CHUNK = 512
 FAR = 1e30
 
 
@@ -166,7 +166,8 @@
     def spans_of(half):
         spans = []
         for slot, length in ((0, BLK), (1, BLK), (2, (half + 1) * edge_rows)):
-            spans += [(slot, start, CHUNK) for start in range(0, length, CHUNK)]
+            size = min(CHUNK, length)
+            spans += [(slot, start, size) for start in range(0, length, size)]
         return spans
 
     for half in range(members // 2):

time: 100 us -> 100 us (level)
  transfers between devices with their start and end apart: 19 -> 19, of which waited for: 9 -> 9; matrix products, arithmetic and copies ran while one was open for 3% -> 3% of each run, Pallas kernels for 25% -> 24%
where the time goes in v2:
time: 100 us; the launch traced here: 99.1 us
  waiting for transfers between devices  40 us (40%)
  starting transfers between devices  25.9 us (26%)
  Pallas kernels  25.7 us (26%)
  other arithmetic  5.3 us (5%)
  between operations  1.24 us (1%)
    ppermute x6, waiting for transfers between devices, along(): return lax.ppermute(tensor, 'seq', route)  31.1 us
    pallas_call x2, Pallas kernels, attend(): pl.pallas_call(functools.partial(attend_kernel, sizes, first), out_shape=...  24.1 us
    ppermute x6, starting transfers between devices, along(): return lax.ppermute(tensor, 'seq', route)  11.8 us
    ppermute x8, starting transfers between devices, previous(): return lax.ppermute(tensor, ('seq', 'pipe'), route)  10.3 us
    ppermute x8, waiting for transfers between devices, previous(): return lax.ppermute(tensor, ('seq', 'pipe'), route)  7.13 us
    ppermute x5, starting transfers between devices, around(): return lax.ppermute(tensor, 'seq', [(i, i ^ hop) for i in range(devices)])  3.8 us
    reduce_sum x1, other arithmetic, on_device(): jnp.sum(out_grads[0].astype(jnp.float32) * outputs[0].astype(jnp.float32)...  2.31 us
  transfers between devices with their start and end apart: 19, of which 9 were waited for; matrix products, arithmetic and copies ran while one was open for 3% of the time, Pallas kernels for 24%

profile of v2, /device:TPU:8, one launch (start us, length us, event | category | flops | bytes accessed | tf_op | source)
XLA Modules:
  0.0 99.1 jit_solution(15856981062116862591)
XLA Ops:
  0.7 0.0 copy-start.4
  0.7 0.0 copy-start.5
  0.7 0.0 copy-start
  0.7 0.0 copy-start.1
  0.7 2.3 %multiply_reduce_fusion = bf16[32,128]{1,0:T(8,128)(2,1)S(1)} fusion(bf16[1,32,128,128]{3,2,1,0:T(8,128)(2,1)} %param.9, bf16[1,32,128,128]{3,2,1,0:T(8,128)(2,1)} %refs_1_.1), kind=kLoop, calls=%fused_computation | loop fusion | flops 2093056 | bytes 2105344 | tf_op jit(solution)/shard_map/reduce_sum | solution.py:353
  3.1 0.0 copy-done.4
  3.1 0.0 copy-done.5
  3.1 0.7 dynamic-slice_bitcast_fusion.10
  3.8 0.0 copy-done
  3.8 0.0 copy-done.1
  3.8 0.1 dynamic-slice_bitcast_fusion
  3.9 0.0 copy-start.2
  3.9 0.0 copy-start.3
  4.0 0.1 pad_maximum_fusion
  4.0 0.1 collective-permute-start
  4.1 1.6 %collective-permute-start.2 = (bf16[2,128,128]{2,1,0:T(8,128)(2,1)S(1)}, bf16[2,128,128]{2,1,0:T(8,128)(2,1)S(1)}, u32[]{:S(2)}, u32[]{:S(2)}) collective-permute-start(bf16[2,128,128]{2,1,0:T(8,128)(2,1)S(1)} %pad_maximum_fusion.3), channel_id=1, source_target_pairs={{0,6},{2,4},{4,2},{6,0},{8,14},{10,12},{12,10},{14,8},{16,22},{18,... | collective-permute-start | bytes 196616 | tf_op jit(solution)/shard_map/ppermute | solution.py:324
  5.8 0.6 collective-permute-start.1
  6.4 0.9 fusion.2
  7.3 1.5 %collective-permute-start.8 = (bf16[17,128,128]{2,1,0:T(8,128)(2,1)}, bf16[17,128,128]{2,1,0:T(8,128)(2,1)S(1)}, u32[]{:S(2)}, u32[]{:S(2)}) collective-permute-start(bf16[17,128,128]{2,1,0:T(8,128)(2,1)} %fusion.2), channel_id=1, source_target_pairs={{0,4},{2,6},{4,0},{6,2},{8,12},{10,14},{12,8},{14,10},{16,20},{18,... | collective-permute-start | bytes 1671176 | tf_op jit(solution)/shard_map/ppermute | solution.py:324
  8.8 0.0 copy-done.2
  8.8 0.0 copy-done.3
  8.8 0.0 collective-permute-done.refs_3_
  8.8 0.0 collective-permute-done.2
  8.8 1.7 %collective-permute-done.1 = bf16[2,128,128]{2,1,0:T(8,128)(2,1)S(1)} collective-permute-done((bf16[2,128,128]{2,1,0:T(8,128)(2,1)S(1)}, bf16[2,128,128]{2,1,0:T(8,128)(2,1)S(1)}, u32[]{:S(2)}, u32[]{:S(2)}) %collective-permute-start.1) | collective-permute-done | bytes 65568 | tf_op jit(solution)/shard_map/ppermute | solution.py:324
  10.5 3.5 %collective-permute-start.3 = (bf16[2,4,128,128]{3,2,1,0:T(8,128)(2,1)S(1)}, bf16[2,4,128,128]{3,2,1,0:T(8,128)(2,1)}, u32[]{:S(2)}, u32[]{:S(2)}) collective-permute-start(bf16[2,4,128,128]{3,2,1,0:T(8,128)(2,1)S(1)} %pad_maximum_fusion.1.refs_4_), channel_id=1, source_target_pairs={{0,8},{2,10},{4,12},{6,14},{8,16},{10,18},{12,20},{14,22},{16,24},... | collective-permute-start | bytes 786440 | tf_op jit(solution)/shard_map/ppermute | solution.py:329
  14.0 3.0 %collective-permute-start.4 = (bf16[2,4,128,128]{3,2,1,0:T(8,128)(2,1)S(1)}, bf16[2,4,128,128]{3,2,1,0:T(8,128)(2,1)}, u32[]{:S(2)}, u32[]{:S(2)}) collective-permute-start(bf16[2,4,128,128]{3,2,1,0:T(8,128)(2,1)S(1)} %pad_maximum_fusion.1.refs_4_), channel_id=1, source_target_pairs={{0,16},{2,18},{4,20},{6,22},{8,24},{10,26},{12,28},{14,30},{1,17},... | collective-permute-start | bytes 786440 | tf_op jit(solution)/shard_map/ppermute | solution.py:329
  17.1 1.4 %collective-permute-start.5 = (bf16[2,4,128,128]{3,2,1,0:T(8,128)(2,1)S(1)}, bf16[2,4,128,128]{3,2,1,0:T(8,128)(2,1)}, u32[]{:S(2)}, u32[]{:S(2)}) collective-permute-start(bf16[2,4,128,128]{3,2,1,0:T(8,128)(2,1)S(1)} %pad_maximum_fusion.1.refs_4_), channel_id=1, source_target_pairs={{0,24},{2,26},{4,28},{6,30},{1,25},{3,27},{5,29},{7,31}} | collective-permute-start | bytes 786440 | tf_op jit(solution)/shard_map/ppermute | solution.py:329
  18.4 0.9 fusion.3
  19.3 0.0 collective-permute-start.9
  19.3 0.9 fusion.10
  20.2 0.1 pad_add_fusion.meta
  20.3 11.7 %collective-permute-done.3.refs_5_ = bf16[2,4,128,128]{3,2,1,0:T(8,128)(2,1)} collective-permute-done((bf16[2,4,128,128]{3,2,1,0:T(8,128)(2,1)S(1)}, bf16[2,4,128,128]{3,2,1,0:T(8,128)(2,1)}, u32[]{:S(2)}, u32[]{:S(2)}) %collective-permute-start.3) | collective-permute-done | bytes 262176 | tf_op jit(solution)/shard_map/ppermute | solution.py:329
  32.0 3.2 %collective-permute-done.4.refs_6_ = bf16[2,4,128,128]{3,2,1,0:T(8,128)(2,1)} collective-permute-done((bf16[2,4,128,128]{3,2,1,0:T(8,128)(2,1)S(1)}, bf16[2,4,128,128]{3,2,1,0:T(8,128)(2,1)}, u32[]{:S(2)}, u32[]{:S(2)}) %collective-permute-start.4) | collective-permute-done | bytes 262176 | tf_op jit(solution)/shard_map/ppermute | solution.py:329
  35.2 0.0 collective-permute-done.5.refs_7_
  35.2 10.8 %shard_map.85 = (bf16[8,128,128]{2,1,0:T(8,128)(2,1)S(1)}, bf16[8,128,128]{2,1,0:T(8,128)(2,1)S(1)}, f32[1536,128]{1,0:T(8,128)S(1)}, f32[1536,128]{1,0:T(8,128)S(1)}) custom-call(s32[3]{0:T(128)S(1)} %pad_add_fusion.meta, bf16[1,32,128,128]{3,2,1,0:T(8,128)(2,1)S(1)} %copy-done.1, bf16[1,32,128,128]{3,2,1,0:T(8,128)(2,1)S(1)} %copy-done, ...), custom_call_target="tpu_custom_call" | custom-call | flops 3690987520 | bytes 6291456 | tf_op jit(solution)/shard_map/pallas_call | solution.py:262
  46.0 1.3 %collective-permute-start.6 = (bf16[8,128,128]{2,1,0:T(8,128)(2,1)S(1)}, bf16[8,128,128]{2,1,0:T(8,128)(2,1)S(1)}, u32[]{:S(2)}, u32[]{:S(2)}) collective-permute-start(bf16[8,128,128]{2,1,0:T(8,128)(2,1)S(1)} %get-tuple-element.20), channel_id=1, source_target_pairs={{1,0},{3,2},{5,4},{7,6},{9,8},{11,10},{13,12},{15,14},{17,16},{19,... | collective-permute-start | bytes 786440 | tf_op jit(solution)/shard_map/ppermute | solution.py:337
  47.3 1.3 %collective-permute-start.7 = (bf16[8,128,128]{2,1,0:T(8,128)(2,1)S(1)}, bf16[8,128,128]{2,1,0:T(8,128)(2,1)S(1)}, u32[]{:S(2)}, u32[]{:S(2)}) collective-permute-start(bf16[8,128,128]{2,1,0:T(8,128)(2,1)S(1)} %get-tuple-element.21), channel_id=1, source_target_pairs={{1,2},{3,0},{5,6},{7,4},{9,10},{11,8},{13,14},{15,12},{17,18},{19,... | collective-permute-start | bytes 786440 | tf_op jit(solution)/shard_map/ppermute | solution.py:337
  48.6 0.0 collective-permute-done.8.refs_0_
  48.6 0.0 collective-permute-done.9.refs_1_
  48.6 13.3 %shard_map.86 = (bf16[8,128,128]{2,1,0:T(8,128)(2,1)S(1)}, bf16[8,128,128]{2,1,0:T(8,128)(2,1)S(1)}, bf16[2,4,128,128]{3,2,1,0:T(8,128)(2,1)S(1)}, bf16[2,4,128,...) custom-call(s32[3]{0:T(128)S(1)} %pad_add_fusion.meta, ...), custom_call_target="tpu_custom_call" | custom-call | flops 3690987520 | bytes 6291456 | tf_op jit(solution)/shard_map/pallas_call | solution.py:262
  62.0 0.0 collective-permute-done.6.refs_0_
  62.0 0.0 collective-permute-done.7.refs_1_
  62.0 0.7 collective-permute-start.14
  62.8 1.3 %collective-permute-start.13 = (bf16[2,4,128,128]{3,2,0,1:T(8,128)(2,1)S(1)}, bf16[2,4,128,128]{3,2,0,1:T(8,128)(2,1)S(1)}, u32[]{:S(2)}, u32[]{:S(2)}) collective-permute-start(bf16[2,4,128,128]{3,2,0,1:T(8,128)(2,1)S(1)} %copy.11), channel_id=1, source_target_pairs={{16,0},{18,2},{20,4},{22,6},{24,8},{26,10},{28,12},{30,14},{17,1},... | collective-permute-start | bytes 786440 | tf_op jit(solution)/shard_map/ppermute | solution.py:329
  64.1 1.9 %collective-permute-start.12 = (bf16[2,4,128,128]{3,2,0,1:T(8,128)(2,1)S(1)}, bf16[2,4,128,128]{3,2,0,1:T(8,128)(2,1)S(1)}, u32[]{:S(2)}, u32[]{:S(2)}) collective-permute-start(bf16[2,4,128,128]{3,2,0,1:T(8,128)(2,1)S(1)} %copy.9), channel_id=1, source_target_pairs={{8,0},{10,2},{12,4},{14,6},{16,8},{18,10},{20,12},{22,14},{24,16},... | collective-permute-start | bytes 786440 | tf_op jit(solution)/shard_map/ppermute | solution.py:329
  66.0 1.3 %collective-permute-start.10 = (bf16[8,128,128]{2,1,0:T(8,128)(2,1)S(1)}, bf16[8,128,128]{2,1,0:T(8,128)(2,1)S(1)}, u32[]{:S(2)}, u32[]{:S(2)}) collective-permute-start(bf16[8,128,128]{2,1,0:T(8,128)(2,1)S(1)} %get-tuple-element.31), channel_id=1, source_target_pairs={{1,4},{3,6},{5,0},{7,2},{9,12},{11,14},{13,8},{15,10},{17,20},{19,... | collective-permute-start | bytes 786440 | tf_op jit(solution)/shard_map/ppermute | solution.py:337
  67.3 1.3 %collective-permute-start.11 = (bf16[8,128,128]{2,1,0:T(8,128)(2,1)S(1)}, bf16[8,128,128]{2,1,0:T(8,128)(2,1)S(1)}, u32[]{:S(2)}, u32[]{:S(2)}) collective-permute-start(bf16[8,128,128]{2,1,0:T(8,128)(2,1)S(1)} %get-tuple-element.32), channel_id=1, source_target_pairs={{1,6},{3,4},{5,2},{7,0},{9,14},{11,12},{13,10},{15,8},{17,22},{19,... | collective-permute-start | bytes 786440 | tf_op jit(solution)/shard_map/ppermute | solution.py:337
  68.6 0.0 collective-permute-done.14
  68.6 11.0 %collective-permute-done.13 = bf16[2,4,128,128]{3,2,0,1:T(8,128)(2,1)S(1)} collective-permute-done((bf16[2,4,128,128]{3,2,0,1:T(8,128)(2,1)S(1)}, bf16[2,4,128,128]{3,2,0,1:T(8,128)(2,1)S(1)}, u32[]{:S(2)}, u32[]{:S(2)}) %collective-permute-start.13) | collective-permute-done | bytes 262176 | tf_op jit(solution)/shard_map/ppermute | solution.py:329
  79.6 5.2 %collective-permute-done.12 = bf16[2,4,128,128]{3,2,0,1:T(8,128)(2,1)S(1)} collective-permute-done((bf16[2,4,128,128]{3,2,0,1:T(8,128)(2,1)S(1)}, bf16[2,4,128,128]{3,2,0,1:T(8,128)(2,1)S(1)}, u32[]{:S(2)}, u32[]{:S(2)}) %collective-permute-start.12) | collective-permute-done | bytes 262176 | tf_op jit(solution)/shard_map/ppermute | solution.py:329
  84.8 0.1 fusion.6
  85.0 1.3 %collective-permute-start.15 = (bf16[2,128,128]{2,1,0:T(8,128)(2,1)S(1)}, bf16[2,128,128]{2,1,0:T(8,128)(2,1)S(1)}, u32[]{:S(2)}, u32[]{:S(2)}) collective-permute-start(bf16[2,128,128]{2,1,0:T(8,128)(2,1)S(1)} %get-tuple-element.46), channel_id=1, source_target_pairs={{1,0},{3,2},{5,4},{7,6},{9,8},{11,10},{13,12},{15,14},{17,16},{19,... | collective-permute-start | bytes 196616 | tf_op jit(solution)/shard_map/ppermute | solution.py:337
  86.3 1.3 %collective-permute-start.16 = (bf16[2,128,128]{2,1,0:T(8,128)(2,1)S(1)}, bf16[2,128,128]{2,1,0:T(8,128)(2,1)S(1)}, u32[]{:S(2)}, u32[]{:S(2)}) collective-permute-start(bf16[2,128,128]{2,1,0:T(8,128)(2,1)S(1)} %get-tuple-element.45), channel_id=1, source_target_pairs={{1,2},{3,0},{5,6},{7,4},{9,10},{11,8},{13,14},{15,12},{17,18},{19,... | collective-permute-start | bytes 196616 | tf_op jit(solution)/shard_map/ppermute | solution.py:337
  87.6 1.3 %collective-permute-start.17 = (bf16[2,128,128]{2,1,0:T(8,128)(2,1)S(1)}, bf16[2,128,128]{2,1,0:T(8,128)(2,1)S(1)}, u32[]{:S(2)}, u32[]{:S(2)}) collective-permute-start(bf16[2,128,128]{2,1,0:T(8,128)(2,1)S(1)} %get-tuple-element.44), channel_id=1, source_target_pairs={{1,4},{3,6},{5,0},{7,2},{9,12},{11,14},{13,8},{15,10},{17,20},{19,... | collective-permute-start | bytes 196616 | tf_op jit(solution)/shard_map/ppermute | solution.py:337
  88.9 0.0 collective-permute-done.10.refs_2_
  88.9 1.3 %collective-permute-start.18 = (bf16[2,128,128]{2,1,0:T(8,128)(2,1)S(1)}, bf16[2,128,128]{2,1,0:T(8,128)(2,1)S(1)}, u32[]{:S(2)}, u32[]{:S(2)}) collective-permute-start(bf16[2,128,128]{2,1,0:T(8,128)(2,1)S(1)} %get-tuple-element.43), channel_id=1, source_target_pairs={{1,6},{3,4},{5,2},{7,0},{9,14},{11,12},{13,10},{15,8},{17,22},{19,... | collective-permute-start | bytes 196616 | tf_op jit(solution)/shard_map/ppermute | solution.py:337
  90.2 0.0 collective-permute-done.11.refs_3_
  90.2 3.7 %collective-permute-done.15.refs_4_ = bf16[2,128,128]{2,1,0:T(8,128)(2,1)S(1)} collective-permute-done((bf16[2,128,128]{2,1,0:T(8,128)(2,1)S(1)}, bf16[2,128,128]{2,1,0:T(8,128)(2,1)S(1)}, u32[]{:S(2)}, u32[]{:S(2)}) %collective-permute-start.15) | collective-permute-done | bytes 65568 | tf_op jit(solution)/shard_map/ppermute | solution.py:337
  93.9 0.3 collective-permute-done.16.refs_5_
  94.2 2.8 %collective-permute-done.17.refs_6_ = bf16[2,128,128]{2,1,0:T(8,128)(2,1)S(1)} collective-permute-done((bf16[2,128,128]{2,1,0:T(8,128)(2,1)S(1)}, bf16[2,128,128]{2,1,0:T(8,128)(2,1)S(1)}, u32[]{:S(2)}, u32[]{:S(2)}) %collective-permute-start.17) | collective-permute-done | bytes 65568 | tf_op jit(solution)/shard_map/ppermute | solution.py:337
  97.0 0.3 collective-permute-done.18.refs_7_
  97.3 1.6 %shard_map.87 = (bf16[1,32,128,128]{3,2,1,0:T(8,128)(2,1)}, bf16[1,4,128,128]{3,2,1,0:T(8,128)(2,1)}, bf16[1,4,128,128]{3,2,1,0:T(8,128)(2,1)}) custom-call(s32[3]{0:T(128)S(1)} %pad_add_fusion.meta, bf16[8,128,128]{2,1,0:T(8,128)(2,1)S(1)} %collective-permute-done.6.refs_0_, bf16[8,128,128]{2,1,0:T(8,128)(2,1)S(1)} %collective-permute-done.7.refs_1_, ...), custom_call_target="tpu_custom_call" | custom-call | tf_op jit(solution)/shard_map/pallas_call | solution.py:299
  (11 shorter events, 0.2 us)
Async XLA Ops:
  0.7 2.4 %copy-start.4 = (bf16[1,4,128,128]{3,2,1,0:T(8,128)(2,1)S(1)}, bf16[1,4,128,128]{3,2,1,0:T(8,128)(2,1)}, u32[]{:S(2)}) copy-start(bf16[1,4,128,128]{3,2,1,0:T(8,128)(2,1)} %param.8) | copy-start | bytes 393220
  0.7 2.4 %copy-start.5 = (bf16[1,4,128,128]{3,2,1,0:T(8,128)(2,1)S(1)}, bf16[1,4,128,128]{3,2,1,0:T(8,128)(2,1)}, u32[]{:S(2)}) copy-start(bf16[1,4,128,128]{3,2,1,0:T(8,128)(2,1)} %param.7) | copy-start | bytes 393220
  0.7 3.1 %copy-start = (bf16[1,32,128,128]{3,2,1,0:T(8,128)(2,1)S(1)}, bf16[1,32,128,128]{3,2,1,0:T(8,128)(2,1)}, u32[]{:S(2)}) copy-start(bf16[1,32,128,128]{3,2,1,0:T(8,128)(2,1)} %refs_1_.1) | copy-start | bytes 3145732
  0.7 3.1 %copy-start.1 = (bf16[1,32,128,128]{3,2,1,0:T(8,128)(2,1)S(1)}, bf16[1,32,128,128]{3,2,1,0:T(8,128)(2,1)}, u32[]{:S(2)}) copy-start(bf16[1,32,128,128]{3,2,1,0:T(8,128)(2,1)} %refs_0_.1) | copy-start | bytes 3145732
  3.9 4.8 %copy-start.2 = (bf16[1,128,128]{2,1,0:T(8,128)(2,1)S(1)}, bf16[1,128,128]{2,1,0:T(8,128)(2,1)}, u32[]{:S(2)}) copy-start(bf16[1,128,128]{2,1,0:T(8,128)(2,1)} %get-tuple-element.51) | copy-start | bytes 98308
  3.9 4.8 %copy-start.3 = (bf16[1,128,128]{2,1,0:T(8,128)(2,1)S(1)}, bf16[1,128,128]{2,1,0:T(8,128)(2,1)}, u32[]{:S(2)}) copy-start(bf16[1,128,128]{2,1,0:T(8,128)(2,1)} %get-tuple-element.61) | copy-start | bytes 98308
  4.0 4.7 %collective-permute-start = (bf16[19,128,128]{2,1,0:T(8,128)(2,1)S(1)}, bf16[19,128,128]{2,1,0:T(8,128)(2,1)S(1)}, u32[]{:S(2)}, u32[]{:S(2)}) collective-permute-start(bf16[19,128,128]{2,1,0:T(8,128)(2,1)S(1)} %pad_maximum_fusion), channel_id=1, source_target_pairs={{0,2},{2,0},{4,6},{6,4},{8,10},{10,8},{12,14},{14,12},{16,18},{18,... | collective-permute-start | bytes 1867784 | tf_op jit(solution)/shard_map/ppermute | solution.py:324
  4.1 4.7 %collective-permute-start.2 = (bf16[2,128,128]{2,1,0:T(8,128)(2,1)S(1)}, bf16[2,128,128]{2,1,0:T(8,128)(2,1)S(1)}, u32[]{:S(2)}, u32[]{:S(2)}) collective-permute-start(bf16[2,128,128]{2,1,0:T(8,128)(2,1)S(1)} %pad_maximum_fusion.3), channel_id=1, source_target_pairs={{0,6},{2,4},{4,2},{6,0},{8,14},{10,12},{12,10},{14,8},{16,22},{18,... | collective-permute-start | bytes 196616 | tf_op jit(solution)/shard_map/ppermute | solution.py:324
  5.8 4.7 %collective-permute-start.1 = (bf16[2,128,128]{2,1,0:T(8,128)(2,1)S(1)}, bf16[2,128,128]{2,1,0:T(8,128)(2,1)S(1)}, u32[]{:S(2)}, u32[]{:S(2)}) collective-permute-start(bf16[2,128,128]{2,1,0:T(8,128)(2,1)S(1)} %pad_maximum_fusion.2), channel_id=1, source_target_pairs={{0,4},{2,6},{4,0},{6,2},{8,12},{10,14},{12,8},{14,10},{16,20},{18,... | collective-permute-start | bytes 196616 | tf_op jit(solution)/shard_map/ppermute | solution.py:324
  7.3 41.4 %collective-permute-start.8 = (bf16[17,128,128]{2,1,0:T(8,128)(2,1)}, bf16[17,128,128]{2,1,0:T(8,128)(2,1)S(1)}, u32[]{:S(2)}, u32[]{:S(2)}) collective-permute-start(bf16[17,128,128]{2,1,0:T(8,128)(2,1)} %fusion.2), channel_id=1, source_target_pairs={{0,4},{2,6},{4,0},{6,2},{8,12},{10,14},{12,8},{14,10},{16,20},{18,... | collective-permute-start | bytes 1671176 | tf_op jit(solution)/shard_map/ppermute | solution.py:324
  10.5 21.5 %collective-permute-start.3 = (bf16[2,4,128,128]{3,2,1,0:T(8,128)(2,1)S(1)}, bf16[2,4,128,128]{3,2,1,0:T(8,128)(2,1)}, u32[]{:S(2)}, u32[]{:S(2)}) collective-permute-start(bf16[2,4,128,128]{3,2,1,0:T(8,128)(2,1)S(1)} %pad_maximum_fusion.1.refs_4_), channel_id=1, source_target_pairs={{0,8},{2,10},{4,12},{6,14},{8,16},{10,18},{12,20},{14,22},{16,24},... | collective-permute-start | bytes 786440 | tf_op jit(solution)/shard_map/ppermute | solution.py:329
  14.0 21.2 %collective-permute-start.4 = (bf16[2,4,128,128]{3,2,1,0:T(8,128)(2,1)S(1)}, bf16[2,4,128,128]{3,2,1,0:T(8,128)(2,1)}, u32[]{:S(2)}, u32[]{:S(2)}) collective-permute-start(bf16[2,4,128,128]{3,2,1,0:T(8,128)(2,1)S(1)} %pad_maximum_fusion.1.refs_4_), channel_id=1, source_target_pairs={{0,16},{2,18},{4,20},{6,22},{8,24},{10,26},{12,28},{14,30},{1,17},... | collective-permute-start | bytes 786440 | tf_op jit(solution)/shard_map/ppermute | solution.py:329
  17.1 18.2 %collective-permute-start.5 = (bf16[2,4,128,128]{3,2,1,0:T(8,128)(2,1)S(1)}, bf16[2,4,128,128]{3,2,1,0:T(8,128)(2,1)}, u32[]{:S(2)}, u32[]{:S(2)}) collective-permute-start(bf16[2,4,128,128]{3,2,1,0:T(8,128)(2,1)S(1)} %pad_maximum_fusion.1.refs_4_), channel_id=1, source_target_pairs={{0,24},{2,26},{4,28},{6,30},{1,25},{3,27},{5,29},{7,31}} | collective-permute-start | bytes 786440 | tf_op jit(solution)/shard_map/ppermute | solution.py:329
  19.3 29.3 %collective-permute-start.9 = (bf16[17,128,128]{2,1,0:T(8,128)(2,1)}, bf16[17,128,128]{2,1,0:T(8,128)(2,1)}, u32[]{:S(2)}, u32[]{:S(2)}) collective-permute-start(bf16[17,128,128]{2,1,0:T(8,128)(2,1)} %fusion.3), channel_id=1, source_target_pairs={{0,6},{2,4},{4,2},{6,0},{8,14},{10,12},{12,10},{14,8},{16,22},{18,... | collective-permute-start | bytes 1671176 | tf_op jit(solution)/shard_map/ppermute | solution.py:324
  46.0 16.0 %collective-permute-start.6 = (bf16[8,128,128]{2,1,0:T(8,128)(2,1)S(1)}, bf16[8,128,128]{2,1,0:T(8,128)(2,1)S(1)}, u32[]{:S(2)}, u32[]{:S(2)}) collective-permute-start(bf16[8,128,128]{2,1,0:T(8,128)(2,1)S(1)} %get-tuple-element.20), channel_id=1, source_target_pairs={{1,0},{3,2},{5,4},{7,6},{9,8},{11,10},{13,12},{15,14},{17,16},{19,... | collective-permute-start | bytes 786440 | tf_op jit(solution)/shard_map/ppermute | solution.py:337
  47.3 14.7 %collective-permute-start.7 = (bf16[8,128,128]{2,1,0:T(8,128)(2,1)S(1)}, bf16[8,128,128]{2,1,0:T(8,128)(2,1)S(1)}, u32[]{:S(2)}, u32[]{:S(2)}) collective-permute-start(bf16[8,128,128]{2,1,0:T(8,128)(2,1)S(1)} %get-tuple-element.21), channel_id=1, source_target_pairs={{1,2},{3,0},{5,6},{7,4},{9,10},{11,8},{13,14},{15,12},{17,18},{19,... | collective-permute-start | bytes 786440 | tf_op jit(solution)/shard_map/ppermute | solution.py:337
  62.0 6.6 %collective-permute-start.14 = (bf16[2,4,128,128]{3,2,0,1:T(8,128)(2,1)S(1)}, bf16[2,4,128,128]{3,2,0,1:T(8,128)(2,1)S(1)}, u32[]{:S(2)}, u32[]{:S(2)}) collective-permute-start(bf16[2,4,128,128]{3,2,0,1:T(8,128)(2,1)S(1)} %copy.12), channel_id=1, source_target_pairs={{24,0},{26,2},{28,4},{30,6},{25,1},{27,3},{29,5},{31,7}} | collective-permute-start | bytes 786440 | tf_op jit(solution)/shard_map/ppermute | solution.py:329
  62.8 16.9 %collective-permute-start.13 = (bf16[2,4,128,128]{3,2,0,1:T(8,128)(2,1)S(1)}, bf16[2,4,128,128]{3,2,0,1:T(8,128)(2,1)S(1)}, u32[]{:S(2)}, u32[]{:S(2)}) collective-permute-start(bf16[2,4,128,128]{3,2,0,1:T(8,128)(2,1)S(1)} %copy.11), channel_id=1, source_target_pairs={{16,0},{18,2},{20,4},{22,6},{24,8},{26,10},{28,12},{30,14},{17,1},... | collective-permute-start | bytes 786440 | tf_op jit(solution)/shard_map/ppermute | solution.py:329
  64.1 20.7 %collective-permute-start.12 = (bf16[2,4,128,128]{3,2,0,1:T(8,128)(2,1)S(1)}, bf16[2,4,128,128]{3,2,0,1:T(8,128)(2,1)S(1)}, u32[]{:S(2)}, u32[]{:S(2)}) collective-permute-start(bf16[2,4,128,128]{3,2,0,1:T(8,128)(2,1)S(1)} %copy.9), channel_id=1, source_target_pairs={{8,0},{10,2},{12,4},{14,6},{16,8},{18,10},{20,12},{22,14},{24,16},... | collective-permute-start | bytes 786440 | tf_op jit(solution)/shard_map/ppermute | solution.py:329
  66.0 22.9 %collective-permute-start.10 = (bf16[8,128,128]{2,1,0:T(8,128)(2,1)S(1)}, bf16[8,128,128]{2,1,0:T(8,128)(2,1)S(1)}, u32[]{:S(2)}, u32[]{:S(2)}) collective-permute-start(bf16[8,128,128]{2,1,0:T(8,128)(2,1)S(1)} %get-tuple-element.31), channel_id=1, source_target_pairs={{1,4},{3,6},{5,0},{7,2},{9,12},{11,14},{13,8},{15,10},{17,20},{19,... | collective-permute-start | bytes 786440 | tf_op jit(solution)/shard_map/ppermute | solution.py:337
  67.3 22.9 %collective-permute-start.11 = (bf16[8,128,128]{2,1,0:T(8,128)(2,1)S(1)}, bf16[8,128,128]{2,1,0:T(8,128)(2,1)S(1)}, u32[]{:S(2)}, u32[]{:S(2)}) collective-permute-start(bf16[8,128,128]{2,1,0:T(8,128)(2,1)S(1)} %get-tuple-element.32), channel_id=1, source_target_pairs={{1,6},{3,4},{5,2},{7,0},{9,14},{11,12},{13,10},{15,8},{17,22},{19,... | collective-permute-start | bytes 786440 | tf_op jit(solution)/shard_map/ppermute | solution.py:337
  85.0 8.9 %collective-permute-start.15 = (bf16[2,128,128]{2,1,0:T(8,128)(2,1)S(1)}, bf16[2,128,128]{2,1,0:T(8,128)(2,1)S(1)}, u32[]{:S(2)}, u32[]{:S(2)}) collective-permute-start(bf16[2,128,128]{2,1,0:T(8,128)(2,1)S(1)} %get-tuple-element.46), channel_id=1, source_target_pairs={{1,0},{3,2},{5,4},{7,6},{9,8},{11,10},{13,12},{15,14},{17,16},{19,... | collective-permute-start | bytes 196616 | tf_op jit(solution)/shard_map/ppermute | solution.py:337
  86.3 7.9 %collective-permute-start.16 = (bf16[2,128,128]{2,1,0:T(8,128)(2,1)S(1)}, bf16[2,128,128]{2,1,0:T(8,128)(2,1)S(1)}, u32[]{:S(2)}, u32[]{:S(2)}) collective-permute-start(bf16[2,128,128]{2,1,0:T(8,128)(2,1)S(1)} %get-tuple-element.45), channel_id=1, source_target_pairs={{1,2},{3,0},{5,6},{7,4},{9,10},{11,8},{13,14},{15,12},{17,18},{19,... | collective-permute-start | bytes 196616 | tf_op jit(solution)/shard_map/ppermute | solution.py:337
  87.6 9.4 %collective-permute-start.17 = (bf16[2,128,128]{2,1,0:T(8,128)(2,1)S(1)}, bf16[2,128,128]{2,1,0:T(8,128)(2,1)S(1)}, u32[]{:S(2)}, u32[]{:S(2)}) collective-permute-start(bf16[2,128,128]{2,1,0:T(8,128)(2,1)S(1)} %get-tuple-element.44), channel_id=1, source_target_pairs={{1,4},{3,6},{5,0},{7,2},{9,12},{11,14},{13,8},{15,10},{17,20},{19,... | collective-permute-start | bytes 196616 | tf_op jit(solution)/shard_map/ppermute | solution.py:337
  88.9 8.4 %collective-permute-start.18 = (bf16[2,128,128]{2,1,0:T(8,128)(2,1)S(1)}, bf16[2,128,128]{2,1,0:T(8,128)(2,1)S(1)}, u32[]{:S(2)}, u32[]{:S(2)}) collective-permute-start(bf16[2,128,128]{2,1,0:T(8,128)(2,1)S(1)} %get-tuple-element.43), channel_id=1, source_target_pairs={{1,6},{3,4},{5,2},{7,0},{9,14},{11,12},{13,10},{15,8},{17,22},{19,... | collective-permute-start | bytes 196616 | tf_op jit(solution)/shard_map/ppermute | solution.py:337

commit v3 on v2

--- a/solution.py
+++ b/solution.py
@@ -73,12 +73,14 @@
             (deltas.at[mine], low_buf.at[places[0]]),
         ]
         loads += of_pack(pack, places[1])
-        key_acc[...] = jnp.zeros_like(key_acc)
-        value_acc[...] = jnp.zeros_like(value_acc)
     else:
         loads += of_pack(packs[0], places[0]) + of_pack(packs[1], places[1])
-        loads += [(acc_ins[0], key_acc), (acc_ins[1], value_acc)]
     copies = run(loads, in_sem)
+    if not first:
+        key_more, value_more, more_sem = take[-3:]
+        more_copies = run([(acc_ins[0], key_more), (acc_ins[1], value_more)], more_sem)
+    key_acc[...] = jnp.zeros_like(key_acc)
+    value_acc[...] = jnp.zeros_like(value_acc)
     for slot in range(2):
         for hop in range(reach + 1):
             source = near if hop == 0 else far[hop - 1]
@@ -190,8 +192,12 @@
         for copy in copies:
             copy.wait()
         return
-    far_done, own_done, blank, far_sem = take[15:]
+    far_done, own_done, blank, far_sem = take[15:19]
     copies = run(stores, out_sem)
+    for copy in more_copies:
+        copy.wait()
+    key_acc[...] += key_more[...]
+    value_acc[...] += value_more[...]
     blank[...] = jnp.zeros_like(blank)
     shape = (members, rows, feature)
     for slot in range(2):
@@ -257,6 +263,9 @@
             pltpu.VMEM(pair, wide),
             pltpu.VMEM(pair, low),
             pltpu.SemaphoreType.DMA((reach + 1,)),
+            pltpu.VMEM(acc, wide),
+            pltpu.VMEM(acc, wide),
+            pltpu.SemaphoreType.DMA((2,)),
         ]
     work = heads * 2 * rows * (2 * BLK + 3 * rows)
     return pl.pallas_call(
@@ -269,7 +278,7 @@
         cost_estimate=pl.CostEstimate(
             flops=10 * work * feature, transcendentals=work, bytes_accessed=6 * 1024 * 1024
         ),
-        compiler_params=pltpu.CompilerParams(vmem_limit_bytes=32 * 1024 * 1024),
+        compiler_params=pltpu.CompilerParams(vmem_limit_bytes=22 * 1024 * 1024),
     )(meta, *inputs, near, *far)
 
 

time: 100 us -> 100 us (level)
  transfers between devices with their start and end apart: 19 -> 19, of which waited for: 9 -> 9; matrix products, arithmetic and copies ran while one was open for 3% -> 3% of each run, Pallas kernels for 24% -> 25%
where the time goes in v3:
time: 100 us; the launch traced here: 99.3 us
  waiting for transfers between devices  40 us (40%)
  Pallas kernels  26 us (26%)
  starting transfers between devices  25.9 us (26%)
  other arithmetic  5.3 us (5%)
  between operations  1.24 us (1%)
    ppermute x6, waiting for transfers between devices, along(): return lax.ppermute(tensor, 'seq', route)  31.2 us
    pallas_call x2, Pallas kernels, attend(): pl.pallas_call(functools.partial(attend_kernel, sizes, first), out_shape=...  24.4 us
    ppermute x6, starting transfers between devices, along(): return lax.ppermute(tensor, 'seq', route)  11.8 us
    ppermute x8, starting transfers between devices, previous(): return lax.ppermute(tensor, ('seq', 'pipe'), route)  10.3 us
    ppermute x8, waiting for transfers between devices, previous(): return lax.ppermute(tensor, ('seq', 'pipe'), route)  7.12 us
    ppermute x5, starting transfers between devices, around(): return lax.ppermute(tensor, 'seq', [(i, i ^ hop) for i in range(devices)])  3.8 us
    reduce_sum x1, other arithmetic, on_device(): jnp.sum(out_grads[0].astype(jnp.float32) * outputs[0].astype(jnp.float32)...  2.31 us
  transfers between devices with their start and end apart: 19, of which 9 were waited for; matrix products, arithmetic and copies ran while one was open for 3% of the time, Pallas kernels for 25%

profile of v3, /device:TPU:8, one launch (start us, length us, event | category | flops | bytes accessed | tf_op | source)
XLA Modules:
  0.0 99.3 jit_solution(7273967943214057778)
XLA Ops:
  0.7 0.0 copy-start.4
  0.7 0.0 copy-start.5
  0.7 0.0 copy-start
  0.7 0.0 copy-start.1
  0.7 2.3 %multiply_reduce_fusion = bf16[32,128]{1,0:T(8,128)(2,1)S(1)} fusion(bf16[1,32,128,128]{3,2,1,0:T(8,128)(2,1)} %param.9, bf16[1,32,128,128]{3,2,1,0:T(8,128)(2,1)} %refs_1_.1), kind=kLoop, calls=%fused_computation | loop fusion | flops 2093056 | bytes 2105344 | tf_op jit(solution)/shard_map/reduce_sum | solution.py:362
  3.1 0.0 copy-done.4
  3.1 0.0 copy-done.5
  3.1 0.7 dynamic-slice_bitcast_fusion.10
  3.8 0.0 copy-done
  3.8 0.0 copy-done.1
  3.8 0.1 dynamic-slice_bitcast_fusion
  3.9 0.0 copy-start.2
  3.9 0.0 copy-start.3
  4.0 0.1 pad_maximum_fusion
  4.0 0.1 collective-permute-start
  4.1 1.6 %collective-permute-start.2 = (bf16[2,128,128]{2,1,0:T(8,128)(2,1)S(1)}, bf16[2,128,128]{2,1,0:T(8,128)(2,1)S(1)}, u32[]{:S(2)}, u32[]{:S(2)}) collective-permute-start(bf16[2,128,128]{2,1,0:T(8,128)(2,1)S(1)} %pad_maximum_fusion.3), channel_id=1, source_target_pairs={{0,6},{2,4},{4,2},{6,0},{8,14},{10,12},{12,10},{14,8},{16,22},{18,... | collective-permute-start | bytes 196616 | tf_op jit(solution)/shard_map/ppermute | solution.py:333
  5.8 0.6 collective-permute-start.1
  6.4 0.9 fusion.2
  7.3 1.5 %collective-permute-start.8 = (bf16[17,128,128]{2,1,0:T(8,128)(2,1)}, bf16[17,128,128]{2,1,0:T(8,128)(2,1)S(1)}, u32[]{:S(2)}, u32[]{:S(2)}) collective-permute-start(bf16[17,128,128]{2,1,0:T(8,128)(2,1)} %fusion.2), channel_id=1, source_target_pairs={{0,4},{2,6},{4,0},{6,2},{8,12},{10,14},{12,8},{14,10},{16,20},{18,... | collective-permute-start | bytes 1671176 | tf_op jit(solution)/shard_map/ppermute | solution.py:333
  8.8 0.0 copy-done.2
  8.8 0.0 copy-done.3
  8.8 0.0 collective-permute-done.refs_3_
  8.8 0.0 collective-permute-done.2
  8.8 1.7 %collective-permute-done.1 = bf16[2,128,128]{2,1,0:T(8,128)(2,1)S(1)} collective-permute-done((bf16[2,128,128]{2,1,0:T(8,128)(2,1)S(1)}, bf16[2,128,128]{2,1,0:T(8,128)(2,1)S(1)}, u32[]{:S(2)}, u32[]{:S(2)}) %collective-permute-start.1) | collective-permute-done | bytes 65568 | tf_op jit(solution)/shard_map/ppermute | solution.py:333
  10.5 3.5 %collective-permute-start.3 = (bf16[2,4,128,128]{3,2,1,0:T(8,128)(2,1)S(1)}, bf16[2,4,128,128]{3,2,1,0:T(8,128)(2,1)}, u32[]{:S(2)}, u32[]{:S(2)}) collective-permute-start(bf16[2,4,128,128]{3,2,1,0:T(8,128)(2,1)S(1)} %pad_maximum_fusion.1.refs_4_), channel_id=1, source_target_pairs={{0,8},{2,10},{4,12},{6,14},{8,16},{10,18},{12,20},{14,22},{16,24},... | collective-permute-start | bytes 786440 | tf_op jit(solution)/shard_map/ppermute | solution.py:338
  14.0 3.0 %collective-permute-start.4 = (bf16[2,4,128,128]{3,2,1,0:T(8,128)(2,1)S(1)}, bf16[2,4,128,128]{3,2,1,0:T(8,128)(2,1)}, u32[]{:S(2)}, u32[]{:S(2)}) collective-permute-start(bf16[2,4,128,128]{3,2,1,0:T(8,128)(2,1)S(1)} %pad_maximum_fusion.1.refs_4_), channel_id=1, source_target_pairs={{0,16},{2,18},{4,20},{6,22},{8,24},{10,26},{12,28},{14,30},{1,17},... | collective-permute-start | bytes 786440 | tf_op jit(solution)/shard_map/ppermute | solution.py:338
  17.1 1.4 %collective-permute-start.5 = (bf16[2,4,128,128]{3,2,1,0:T(8,128)(2,1)S(1)}, bf16[2,4,128,128]{3,2,1,0:T(8,128)(2,1)}, u32[]{:S(2)}, u32[]{:S(2)}) collective-permute-start(bf16[2,4,128,128]{3,2,1,0:T(8,128)(2,1)S(1)} %pad_maximum_fusion.1.refs_4_), channel_id=1, source_target_pairs={{0,24},{2,26},{4,28},{6,30},{1,25},{3,27},{5,29},{7,31}} | collective-permute-start | bytes 786440 | tf_op jit(solution)/shard_map/ppermute | solution.py:338
  18.4 0.9 fusion.3
  19.3 0.0 collective-permute-start.9
  19.3 0.9 fusion.10
  20.2 0.1 pad_add_fusion.meta
  20.3 11.7 %collective-permute-done.3.refs_5_ = bf16[2,4,128,128]{3,2,1,0:T(8,128)(2,1)} collective-permute-done((bf16[2,4,128,128]{3,2,1,0:T(8,128)(2,1)S(1)}, bf16[2,4,128,128]{3,2,1,0:T(8,128)(2,1)}, u32[]{:S(2)}, u32[]{:S(2)}) %collective-permute-start.3) | collective-permute-done | bytes 262176 | tf_op jit(solution)/shard_map/ppermute | solution.py:338
  32.0 3.2 %collective-permute-done.4.refs_6_ = bf16[2,4,128,128]{3,2,1,0:T(8,128)(2,1)} collective-permute-done((bf16[2,4,128,128]{3,2,1,0:T(8,128)(2,1)S(1)}, bf16[2,4,128,128]{3,2,1,0:T(8,128)(2,1)}, u32[]{:S(2)}, u32[]{:S(2)}) %collective-permute-start.4) | collective-permute-done | bytes 262176 | tf_op jit(solution)/shard_map/ppermute | solution.py:338
  35.2 0.0 collective-permute-done.5.refs_7_
  35.2 10.8 %shard_map.85 = (bf16[8,128,128]{2,1,0:T(8,128)(2,1)S(1)}, bf16[8,128,128]{2,1,0:T(8,128)(2,1)S(1)}, f32[1536,128]{1,0:T(8,128)S(1)}, f32[1536,128]{1,0:T(8,128)S(1)}) custom-call(s32[3]{0:T(128)S(1)} %pad_add_fusion.meta, bf16[1,32,128,128]{3,2,1,0:T(8,128)(2,1)S(1)} %copy-done.1, bf16[1,32,128,128]{3,2,1,0:T(8,128)(2,1)S(1)} %copy-done, ...), custom_call_target="tpu_custom_call" | custom-call | flops 3690987520 | bytes 6291456 | tf_op jit(solution)/shard_map/pallas_call | solution.py:271
  46.0 1.3 %collective-permute-start.6 = (bf16[8,128,128]{2,1,0:T(8,128)(2,1)S(1)}, bf16[8,128,128]{2,1,0:T(8,128)(2,1)S(1)}, u32[]{:S(2)}, u32[]{:S(2)}) collective-permute-start(bf16[8,128,128]{2,1,0:T(8,128)(2,1)S(1)} %get-tuple-element.20), channel_id=1, source_target_pairs={{1,0},{3,2},{5,4},{7,6},{9,8},{11,10},{13,12},{15,14},{17,16},{19,... | collective-permute-start | bytes 786440 | tf_op jit(solution)/shard_map/ppermute | solution.py:346
  47.3 1.3 %collective-permute-start.7 = (bf16[8,128,128]{2,1,0:T(8,128)(2,1)S(1)}, bf16[8,128,128]{2,1,0:T(8,128)(2,1)S(1)}, u32[]{:S(2)}, u32[]{:S(2)}) collective-permute-start(bf16[8,128,128]{2,1,0:T(8,128)(2,1)S(1)} %get-tuple-element.21), channel_id=1, source_target_pairs={{1,2},{3,0},{5,6},{7,4},{9,10},{11,8},{13,14},{15,12},{17,18},{19,... | collective-permute-start | bytes 786440 | tf_op jit(solution)/shard_map/ppermute | solution.py:346
  48.6 0.0 collective-permute-done.8.refs_0_
  48.6 0.0 collective-permute-done.9.refs_1_
  48.6 13.6 %shard_map.86 = (bf16[8,128,128]{2,1,0:T(8,128)(2,1)S(1)}, bf16[8,128,128]{2,1,0:T(8,128)(2,1)S(1)}, bf16[2,4,128,128]{3,2,1,0:T(8,128)(2,1)S(1)}, bf16[2,4,128,...) custom-call(s32[3]{0:T(128)S(1)} %pad_add_fusion.meta, ...), custom_call_target="tpu_custom_call" | custom-call | flops 3690987520 | bytes 6291456 | tf_op jit(solution)/shard_map/pallas_call | solution.py:271
  62.2 0.0 collective-permute-done.6.refs_0_
  62.2 0.0 collective-permute-done.7.refs_1_
  62.3 0.7 collective-permute-start.14
  63.0 1.3 %collective-permute-start.13 = (bf16[2,4,128,128]{3,2,0,1:T(8,128)(2,1)S(1)}, bf16[2,4,128,128]{3,2,0,1:T(8,128)(2,1)S(1)}, u32[]{:S(2)}, u32[]{:S(2)}) collective-permute-start(bf16[2,4,128,128]{3,2,0,1:T(8,128)(2,1)S(1)} %copy.11), channel_id=1, source_target_pairs={{16,0},{18,2},{20,4},{22,6},{24,8},{26,10},{28,12},{30,14},{17,1},... | collective-permute-start | bytes 786440 | tf_op jit(solution)/shard_map/ppermute | solution.py:338
  64.3 1.9 %collective-permute-start.12 = (bf16[2,4,128,128]{3,2,0,1:T(8,128)(2,1)S(1)}, bf16[2,4,128,128]{3,2,0,1:T(8,128)(2,1)S(1)}, u32[]{:S(2)}, u32[]{:S(2)}) collective-permute-start(bf16[2,4,128,128]{3,2,0,1:T(8,128)(2,1)S(1)} %copy.9), channel_id=1, source_target_pairs={{8,0},{10,2},{12,4},{14,6},{16,8},{18,10},{20,12},{22,14},{24,16},... | collective-permute-start | bytes 786440 | tf_op jit(solution)/shard_map/ppermute | solution.py:338
  66.2 1.3 %collective-permute-start.10 = (bf16[8,128,128]{2,1,0:T(8,128)(2,1)S(1)}, bf16[8,128,128]{2,1,0:T(8,128)(2,1)S(1)}, u32[]{:S(2)}, u32[]{:S(2)}) collective-permute-start(bf16[8,128,128]{2,1,0:T(8,128)(2,1)S(1)} %get-tuple-element.31), channel_id=1, source_target_pairs={{1,4},{3,6},{5,0},{7,2},{9,12},{11,14},{13,8},{15,10},{17,20},{19,... | collective-permute-start | bytes 786440 | tf_op jit(solution)/shard_map/ppermute | solution.py:346
  67.5 1.3 %collective-permute-start.11 = (bf16[8,128,128]{2,1,0:T(8,128)(2,1)S(1)}, bf16[8,128,128]{2,1,0:T(8,128)(2,1)S(1)}, u32[]{:S(2)}, u32[]{:S(2)}) collective-permute-start(bf16[8,128,128]{2,1,0:T(8,128)(2,1)S(1)} %get-tuple-element.32), channel_id=1, source_target_pairs={{1,6},{3,4},{5,2},{7,0},{9,14},{11,12},{13,10},{15,8},{17,22},{19,... | collective-permute-start | bytes 786440 | tf_op jit(solution)/shard_map/ppermute | solution.py:346
  68.8 0.0 collective-permute-done.14
  68.9 11.0 %collective-permute-done.13 = bf16[2,4,128,128]{3,2,0,1:T(8,128)(2,1)S(1)} collective-permute-done((bf16[2,4,128,128]{3,2,0,1:T(8,128)(2,1)S(1)}, bf16[2,4,128,128]{3,2,0,1:T(8,128)(2,1)S(1)}, u32[]{:S(2)}, u32[]{:S(2)}) %collective-permute-start.13) | collective-permute-done | bytes 262176 | tf_op jit(solution)/shard_map/ppermute | solution.py:338
  79.9 5.2 %collective-permute-done.12 = bf16[2,4,128,128]{3,2,0,1:T(8,128)(2,1)S(1)} collective-permute-done((bf16[2,4,128,128]{3,2,0,1:T(8,128)(2,1)S(1)}, bf16[2,4,128,128]{3,2,0,1:T(8,128)(2,1)S(1)}, u32[]{:S(2)}, u32[]{:S(2)}) %collective-permute-start.12) | collective-permute-done | bytes 262176 | tf_op jit(solution)/shard_map/ppermute | solution.py:338
  85.1 0.1 fusion.6
  85.2 1.3 %collective-permute-start.15 = (bf16[2,128,128]{2,1,0:T(8,128)(2,1)S(1)}, bf16[2,128,128]{2,1,0:T(8,128)(2,1)S(1)}, u32[]{:S(2)}, u32[]{:S(2)}) collective-permute-start(bf16[2,128,128]{2,1,0:T(8,128)(2,1)S(1)} %get-tuple-element.46), channel_id=1, source_target_pairs={{1,0},{3,2},{5,4},{7,6},{9,8},{11,10},{13,12},{15,14},{17,16},{19,... | collective-permute-start | bytes 196616 | tf_op jit(solution)/shard_map/ppermute | solution.py:346
  86.5 1.3 %collective-permute-start.16 = (bf16[2,128,128]{2,1,0:T(8,128)(2,1)S(1)}, bf16[2,128,128]{2,1,0:T(8,128)(2,1)S(1)}, u32[]{:S(2)}, u32[]{:S(2)}) collective-permute-start(bf16[2,128,128]{2,1,0:T(8,128)(2,1)S(1)} %get-tuple-element.45), channel_id=1, source_target_pairs={{1,2},{3,0},{5,6},{7,4},{9,10},{11,8},{13,14},{15,12},{17,18},{19,... | collective-permute-start | bytes 196616 | tf_op jit(solution)/shard_map/ppermute | solution.py:346
  87.8 1.3 %collective-permute-start.17 = (bf16[2,128,128]{2,1,0:T(8,128)(2,1)S(1)}, bf16[2,128,128]{2,1,0:T(8,128)(2,1)S(1)}, u32[]{:S(2)}, u32[]{:S(2)}) collective-permute-start(bf16[2,128,128]{2,1,0:T(8,128)(2,1)S(1)} %get-tuple-element.44), channel_id=1, source_target_pairs={{1,4},{3,6},{5,0},{7,2},{9,12},{11,14},{13,8},{15,10},{17,20},{19,... | collective-permute-start | bytes 196616 | tf_op jit(solution)/shard_map/ppermute | solution.py:346
  89.1 0.0 collective-permute-done.10.refs_2_
  89.1 1.3 %collective-permute-start.18 = (bf16[2,128,128]{2,1,0:T(8,128)(2,1)S(1)}, bf16[2,128,128]{2,1,0:T(8,128)(2,1)S(1)}, u32[]{:S(2)}, u32[]{:S(2)}) collective-permute-start(bf16[2,128,128]{2,1,0:T(8,128)(2,1)S(1)} %get-tuple-element.43), channel_id=1, source_target_pairs={{1,6},{3,4},{5,2},{7,0},{9,14},{11,12},{13,10},{15,8},{17,22},{19,... | collective-permute-start | bytes 196616 | tf_op jit(solution)/shard_map/ppermute | solution.py:346
  90.4 0.0 collective-permute-done.11.refs_3_
  90.5 3.7 %collective-permute-done.15.refs_4_ = bf16[2,128,128]{2,1,0:T(8,128)(2,1)S(1)} collective-permute-done((bf16[2,128,128]{2,1,0:T(8,128)(2,1)S(1)}, bf16[2,128,128]{2,1,0:T(8,128)(2,1)S(1)}, u32[]{:S(2)}, u32[]{:S(2)}) %collective-permute-start.15) | collective-permute-done | bytes 65568 | tf_op jit(solution)/shard_map/ppermute | solution.py:346
  94.1 0.3 collective-permute-done.16.refs_5_
  94.4 2.8 %collective-permute-done.17.refs_6_ = bf16[2,128,128]{2,1,0:T(8,128)(2,1)S(1)} collective-permute-done((bf16[2,128,128]{2,1,0:T(8,128)(2,1)S(1)}, bf16[2,128,128]{2,1,0:T(8,128)(2,1)S(1)}, u32[]{:S(2)}, u32[]{:S(2)}) %collective-permute-start.17) | collective-permute-done | bytes 65568 | tf_op jit(solution)/shard_map/ppermute | solution.py:346
  97.3 0.3 collective-permute-done.18.refs_7_
  97.6 1.6 %shard_map.87 = (bf16[1,32,128,128]{3,2,1,0:T(8,128)(2,1)}, bf16[1,4,128,128]{3,2,1,0:T(8,128)(2,1)}, bf16[1,4,128,128]{3,2,1,0:T(8,128)(2,1)}) custom-call(s32[3]{0:T(128)S(1)} %pad_add_fusion.meta, bf16[8,128,128]{2,1,0:T(8,128)(2,1)S(1)} %collective-permute-done.6.refs_0_, bf16[8,128,128]{2,1,0:T(8,128)(2,1)S(1)} %collective-permute-done.7.refs_1_, ...), custom_call_target="tpu_custom_call" | custom-call | tf_op jit(solution)/shard_map/pallas_call | solution.py:308
  (11 shorter events, 0.2 us)
Async XLA Ops:
  0.7 2.4 %copy-start.4 = (bf16[1,4,128,128]{3,2,1,0:T(8,128)(2,1)S(1)}, bf16[1,4,128,128]{3,2,1,0:T(8,128)(2,1)}, u32[]{:S(2)}) copy-start(bf16[1,4,128,128]{3,2,1,0:T(8,128)(2,1)} %param.8) | copy-start | bytes 393220
  0.7 2.4 %copy-start.5 = (bf16[1,4,128,128]{3,2,1,0:T(8,128)(2,1)S(1)}, bf16[1,4,128,128]{3,2,1,0:T(8,128)(2,1)}, u32[]{:S(2)}) copy-start(bf16[1,4,128,128]{3,2,1,0:T(8,128)(2,1)} %param.7) | copy-start | bytes 393220
  0.7 3.1 %copy-start = (bf16[1,32,128,128]{3,2,1,0:T(8,128)(2,1)S(1)}, bf16[1,32,128,128]{3,2,1,0:T(8,128)(2,1)}, u32[]{:S(2)}) copy-start(bf16[1,32,128,128]{3,2,1,0:T(8,128)(2,1)} %refs_1_.1) | copy-start | bytes 3145732
  0.7 3.1 %copy-start.1 = (bf16[1,32,128,128]{3,2,1,0:T(8,128)(2,1)S(1)}, bf16[1,32,128,128]{3,2,1,0:T(8,128)(2,1)}, u32[]{:S(2)}) copy-start(bf16[1,32,128,128]{3,2,1,0:T(8,128)(2,1)} %refs_0_.1) | copy-start | bytes 3145732
  3.9 4.8 %copy-start.2 = (bf16[1,128,128]{2,1,0:T(8,128)(2,1)S(1)}, bf16[1,128,128]{2,1,0:T(8,128)(2,1)}, u32[]{:S(2)}) copy-start(bf16[1,128,128]{2,1,0:T(8,128)(2,1)} %get-tuple-element.51) | copy-start | bytes 98308
  3.9 4.8 %copy-start.3 = (bf16[1,128,128]{2,1,0:T(8,128)(2,1)S(1)}, bf16[1,128,128]{2,1,0:T(8,128)(2,1)}, u32[]{:S(2)}) copy-start(bf16[1,128,128]{2,1,0:T(8,128)(2,1)} %get-tuple-element.61) | copy-start | bytes 98308
  4.0 4.7 %collective-permute-start = (bf16[19,128,128]{2,1,0:T(8,128)(2,1)S(1)}, bf16[19,128,128]{2,1,0:T(8,128)(2,1)S(1)}, u32[]{:S(2)}, u32[]{:S(2)}) collective-permute-start(bf16[19,128,128]{2,1,0:T(8,128)(2,1)S(1)} %pad_maximum_fusion), channel_id=1, source_target_pairs={{0,2},{2,0},{4,6},{6,4},{8,10},{10,8},{12,14},{14,12},{16,18},{18,... | collective-permute-start | bytes 1867784 | tf_op jit(solution)/shard_map/ppermute | solution.py:333
  4.1 4.7 %collective-permute-start.2 = (bf16[2,128,128]{2,1,0:T(8,128)(2,1)S(1)}, bf16[2,128,128]{2,1,0:T(8,128)(2,1)S(1)}, u32[]{:S(2)}, u32[]{:S(2)}) collective-permute-start(bf16[2,128,128]{2,1,0:T(8,128)(2,1)S(1)} %pad_maximum_fusion.3), channel_id=1, source_target_pairs={{0,6},{2,4},{4,2},{6,0},{8,14},{10,12},{12,10},{14,8},{16,22},{18,... | collective-permute-start | bytes 196616 | tf_op jit(solution)/shard_map/ppermute | solution.py:333
  5.8 4.7 %collective-permute-start.1 = (bf16[2,128,128]{2,1,0:T(8,128)(2,1)S(1)}, bf16[2,128,128]{2,1,0:T(8,128)(2,1)S(1)}, u32[]{:S(2)}, u32[]{:S(2)}) collective-permute-start(bf16[2,128,128]{2,1,0:T(8,128)(2,1)S(1)} %pad_maximum_fusion.2), channel_id=1, source_target_pairs={{0,4},{2,6},{4,0},{6,2},{8,12},{10,14},{12,8},{14,10},{16,20},{18,... | collective-permute-start | bytes 196616 | tf_op jit(solution)/shard_map/ppermute | solution.py:333
  7.3 41.4 %collective-permute-start.8 = (bf16[17,128,128]{2,1,0:T(8,128)(2,1)}, bf16[17,128,128]{2,1,0:T(8,128)(2,1)S(1)}, u32[]{:S(2)}, u32[]{:S(2)}) collective-permute-start(bf16[17,128,128]{2,1,0:T(8,128)(2,1)} %fusion.2), channel_id=1, source_target_pairs={{0,4},{2,6},{4,0},{6,2},{8,12},{10,14},{12,8},{14,10},{16,20},{18,... | collective-permute-start | bytes 1671176 | tf_op jit(solution)/shard_map/ppermute | solution.py:333
  10.5 21.5 %collective-permute-start.3 = (bf16[2,4,128,128]{3,2,1,0:T(8,128)(2,1)S(1)}, bf16[2,4,128,128]{3,2,1,0:T(8,128)(2,1)}, u32[]{:S(2)}, u32[]{:S(2)}) collective-permute-start(bf16[2,4,128,128]{3,2,1,0:T(8,128)(2,1)S(1)} %pad_maximum_fusion.1.refs_4_), channel_id=1, source_target_pairs={{0,8},{2,10},{4,12},{6,14},{8,16},{10,18},{12,20},{14,22},{16,24},... | collective-permute-start | bytes 786440 | tf_op jit(solution)/shard_map/ppermute | solution.py:338
  14.0 21.2 %collective-permute-start.4 = (bf16[2,4,128,128]{3,2,1,0:T(8,128)(2,1)S(1)}, bf16[2,4,128,128]{3,2,1,0:T(8,128)(2,1)}, u32[]{:S(2)}, u32[]{:S(2)}) collective-permute-start(bf16[2,4,128,128]{3,2,1,0:T(8,128)(2,1)S(1)} %pad_maximum_fusion.1.refs_4_), channel_id=1, source_target_pairs={{0,16},{2,18},{4,20},{6,22},{8,24},{10,26},{12,28},{14,30},{1,17},... | collective-permute-start | bytes 786440 | tf_op jit(solution)/shard_map/ppermute | solution.py:338
  17.1 18.2 %collective-permute-start.5 = (bf16[2,4,128,128]{3,2,1,0:T(8,128)(2,1)S(1)}, bf16[2,4,128,128]{3,2,1,0:T(8,128)(2,1)}, u32[]{:S(2)}, u32[]{:S(2)}) collective-permute-start(bf16[2,4,128,128]{3,2,1,0:T(8,128)(2,1)S(1)} %pad_maximum_fusion.1.refs_4_), channel_id=1, source_target_pairs={{0,24},{2,26},{4,28},{6,30},{1,25},{3,27},{5,29},{7,31}} | collective-permute-start | bytes 786440 | tf_op jit(solution)/shard_map/ppermute | solution.py:338
  19.3 29.3 %collective-permute-start.9 = (bf16[17,128,128]{2,1,0:T(8,128)(2,1)}, bf16[17,128,128]{2,1,0:T(8,128)(2,1)}, u32[]{:S(2)}, u32[]{:S(2)}) collective-permute-start(bf16[17,128,128]{2,1,0:T(8,128)(2,1)} %fusion.3), channel_id=1, source_target_pairs={{0,6},{2,4},{4,2},{6,0},{8,14},{10,12},{12,10},{14,8},{16,22},{18,... | collective-permute-start | bytes 1671176 | tf_op jit(solution)/shard_map/ppermute | solution.py:333
  46.0 16.2 %collective-permute-start.6 = (bf16[8,128,128]{2,1,0:T(8,128)(2,1)S(1)}, bf16[8,128,128]{2,1,0:T(8,128)(2,1)S(1)}, u32[]{:S(2)}, u32[]{:S(2)}) collective-permute-start(bf16[8,128,128]{2,1,0:T(8,128)(2,1)S(1)} %get-tuple-element.20), channel_id=1, source_target_pairs={{1,0},{3,2},{5,4},{7,6},{9,8},{11,10},{13,12},{15,14},{17,16},{19,... | collective-permute-start | bytes 786440 | tf_op jit(solution)/shard_map/ppermute | solution.py:346
  47.3 14.9 %collective-permute-start.7 = (bf16[8,128,128]{2,1,0:T(8,128)(2,1)S(1)}, bf16[8,128,128]{2,1,0:T(8,128)(2,1)S(1)}, u32[]{:S(2)}, u32[]{:S(2)}) collective-permute-start(bf16[8,128,128]{2,1,0:T(8,128)(2,1)S(1)} %get-tuple-element.21), channel_id=1, source_target_pairs={{1,2},{3,0},{5,6},{7,4},{9,10},{11,8},{13,14},{15,12},{17,18},{19,... | collective-permute-start | bytes 786440 | tf_op jit(solution)/shard_map/ppermute | solution.py:346
  62.3 6.6 %collective-permute-start.14 = (bf16[2,4,128,128]{3,2,0,1:T(8,128)(2,1)S(1)}, bf16[2,4,128,128]{3,2,0,1:T(8,128)(2,1)S(1)}, u32[]{:S(2)}, u32[]{:S(2)}) collective-permute-start(bf16[2,4,128,128]{3,2,0,1:T(8,128)(2,1)S(1)} %copy.12), channel_id=1, source_target_pairs={{24,0},{26,2},{28,4},{30,6},{25,1},{27,3},{29,5},{31,7}} | collective-permute-start | bytes 786440 | tf_op jit(solution)/shard_map/ppermute | solution.py:338
  63.0 16.9 %collective-permute-start.13 = (bf16[2,4,128,128]{3,2,0,1:T(8,128)(2,1)S(1)}, bf16[2,4,128,128]{3,2,0,1:T(8,128)(2,1)S(1)}, u32[]{:S(2)}, u32[]{:S(2)}) collective-permute-start(bf16[2,4,128,128]{3,2,0,1:T(8,128)(2,1)S(1)} %copy.11), channel_id=1, source_target_pairs={{16,0},{18,2},{20,4},{22,6},{24,8},{26,10},{28,12},{30,14},{17,1},... | collective-permute-start | bytes 786440 | tf_op jit(solution)/shard_map/ppermute | solution.py:338
  64.3 20.8 %collective-permute-start.12 = (bf16[2,4,128,128]{3,2,0,1:T(8,128)(2,1)S(1)}, bf16[2,4,128,128]{3,2,0,1:T(8,128)(2,1)S(1)}, u32[]{:S(2)}, u32[]{:S(2)}) collective-permute-start(bf16[2,4,128,128]{3,2,0,1:T(8,128)(2,1)S(1)} %copy.9), channel_id=1, source_target_pairs={{8,0},{10,2},{12,4},{14,6},{16,8},{18,10},{20,12},{22,14},{24,16},... | collective-permute-start | bytes 786440 | tf_op jit(solution)/shard_map/ppermute | solution.py:338
  66.2 22.9 %collective-permute-start.10 = (bf16[8,128,128]{2,1,0:T(8,128)(2,1)S(1)}, bf16[8,128,128]{2,1,0:T(8,128)(2,1)S(1)}, u32[]{:S(2)}, u32[]{:S(2)}) collective-permute-start(bf16[8,128,128]{2,1,0:T(8,128)(2,1)S(1)} %get-tuple-element.31), channel_id=1, source_target_pairs={{1,4},{3,6},{5,0},{7,2},{9,12},{11,14},{13,8},{15,10},{17,20},{19,... | collective-permute-start | bytes 786440 | tf_op jit(solution)/shard_map/ppermute | solution.py:346
  67.5 22.9 %collective-permute-start.11 = (bf16[8,128,128]{2,1,0:T(8,128)(2,1)S(1)}, bf16[8,128,128]{2,1,0:T(8,128)(2,1)S(1)}, u32[]{:S(2)}, u32[]{:S(2)}) collective-permute-start(bf16[8,128,128]{2,1,0:T(8,128)(2,1)S(1)} %get-tuple-element.32), channel_id=1, source_target_pairs={{1,6},{3,4},{5,2},{7,0},{9,14},{11,12},{13,10},{15,8},{17,22},{19,... | collective-permute-start | bytes 786440 | tf_op jit(solution)/shard_map/ppermute | solution.py:346
  85.2 8.9 %collective-permute-start.15 = (bf16[2,128,128]{2,1,0:T(8,128)(2,1)S(1)}, bf16[2,128,128]{2,1,0:T(8,128)(2,1)S(1)}, u32[]{:S(2)}, u32[]{:S(2)}) collective-permute-start(bf16[2,128,128]{2,1,0:T(8,128)(2,1)S(1)} %get-tuple-element.46), channel_id=1, source_target_pairs={{1,0},{3,2},{5,4},{7,6},{9,8},{11,10},{13,12},{15,14},{17,16},{19,... | collective-permute-start | bytes 196616 | tf_op jit(solution)/shard_map/ppermute | solution.py:346
  86.5 7.9 %collective-permute-start.16 = (bf16[2,128,128]{2,1,0:T(8,128)(2,1)S(1)}, bf16[2,128,128]{2,1,0:T(8,128)(2,1)S(1)}, u32[]{:S(2)}, u32[]{:S(2)}) collective-permute-start(bf16[2,128,128]{2,1,0:T(8,128)(2,1)S(1)} %get-tuple-element.45), channel_id=1, source_target_pairs={{1,2},{3,0},{5,6},{7,4},{9,10},{11,8},{13,14},{15,12},{17,18},{19,... | collective-permute-start | bytes 196616 | tf_op jit(solution)/shard_map/ppermute | solution.py:346
  87.8 9.4 %collective-permute-start.17 = (bf16[2,128,128]{2,1,0:T(8,128)(2,1)S(1)}, bf16[2,128,128]{2,1,0:T(8,128)(2,1)S(1)}, u32[]{:S(2)}, u32[]{:S(2)}) collective-permute-start(bf16[2,128,128]{2,1,0:T(8,128)(2,1)S(1)} %get-tuple-element.44), channel_id=1, source_target_pairs={{1,4},{3,6},{5,0},{7,2},{9,12},{11,14},{13,8},{15,10},{17,20},{19,... | collective-permute-start | bytes 196616 | tf_op jit(solution)/shard_map/ppermute | solution.py:346
  89.1 8.4 %collective-permute-start.18 = (bf16[2,128,128]{2,1,0:T(8,128)(2,1)S(1)}, bf16[2,128,128]{2,1,0:T(8,128)(2,1)S(1)}, u32[]{:S(2)}, u32[]{:S(2)}) collective-permute-start(bf16[2,128,128]{2,1,0:T(8,128)(2,1)S(1)} %get-tuple-element.43), channel_id=1, source_target_pairs={{1,6},{3,4},{5,2},{7,0},{9,14},{11,12},{13,10},{15,8},{17,22},{19,... | collective-permute-start | bytes 196616 | tf_op jit(solution)/shard_map/ppermute | solution.py:346
